TPU v7x, 128 devices: a whole 4x4x4 slice. The times are simulated.
128 devices in a mesh: dp: 8 (over z, y_hi), head: 16 (over y_lo, x, core).
Axes of the slice: x: 4, y: 4 (y_hi: 2, y_lo: 2; y = y_hi * 2 + y_lo), z: 4, core: 2. Of those that a mesh axis runs over, the one named last changes fastest.
Arguments:
- ckpt_query: bfloat16 [4, 8192, 8192], P(None, ('dp', 'head')), may hold values from -0.125 to 0.125
- ckpt_key: bfloat16 [4, 8192, 1024], P(None, ('dp', 'head')), may hold values from -0.125 to 0.125
- ckpt_value: bfloat16 [4, 8192, 1024], P(None, ('dp', 'head')), may hold values from -0.125 to 0.125
- ckpt_output: bfloat16 [4, 8192, 8192], P(None, ('head', 'dp')), may hold values from -0.125 to 0.125
- hidden_in: bfloat16 [4096, 8192], P('dp'), may hold values from -17 to 17
- segment_ids: int32 [8, 512], P('dp'), may hold values from 0 to 3, never falling along the last dimension, each value on 1 to 256 neighbouring positions
Outputs:
- attn_out: bfloat16 [4096, 8192], P('dp', 'head')
All inputs are finite; a program needn't handle non-finite values.
Results may differ from a plain program's by a relative error of at most 0.01.
The roundings to bfloat16 on the way count: a program that leaves them out, or rounds other values in their place, can miss the bound.
Values may be sent and summed in bfloat16 or wider, within the bound.
A program may use at most 128 MiB of HBM per device.

v0:
```python
import jax
import jax.numpy as jnp
from jax import lax
from jax.sharding import PartitionSpec as P

rope_base = 500000.0


def from_partner(value, axis, apart):
    mask = 2**apart
    pairs = [(source, source ^ mask) for source in range(lax.axis_size(axis))]
    return lax.ppermute(value, axis, pairs)


def average(stack):
    return (jnp.sum(stack.astype(jnp.float32), axis=0) * 0.25).astype(jnp.bfloat16)


def rotate(values, positions):
    half = values.shape[-1] // 2
    freq = rope_base ** (-2.0 * jnp.arange(half, dtype=jnp.float32) / values.shape[-1])
    angle = positions[:, None] * freq[None, :]
    cosine = jnp.cos(angle)[:, None, :]
    sine = jnp.sin(angle)[:, None, :]
    first = values[..., :half]
    second = values[..., half:]
    return jnp.concatenate(
        [first * cosine - second * sine, second * cosine + first * sine], axis=-1
    )


def shards(ckpt_query, ckpt_key, ckpt_value, ckpt_output, hidden_in, segment_ids):
    output_weight = None
    moved = (
        lax.all_to_all(ckpt_query, "head", split_axis=2, concat_axis=1, tiled=True),
        lax.all_to_all(ckpt_key, "head", split_axis=2, concat_axis=1, tiled=True),
        lax.all_to_all(ckpt_value, "head", split_axis=2, concat_axis=1, tiled=True),
        lax.all_to_all(ckpt_output, "head", split_axis=2, concat_axis=1, tiled=True),
    )
    output_weight = average(moved[3])
    query_weight = average(moved[0])
    key_weight = average(moved[1])
    value_weight = average(moved[2])
    position = lax.axis_index("head")
    other_key, other_value = from_partner((key_weight, value_weight), "head", 0)
    lower = position // (1 << 0) % 2 == 0
    key_weight = jnp.where(
        lower,
        jnp.concatenate([key_weight, other_key], 1),
        jnp.concatenate([other_key, key_weight], 1),
    )
    value_weight = jnp.where(
        lower,
        jnp.concatenate([value_weight, other_value], 1),
        jnp.concatenate([other_value, value_weight], 1),
    )
    tok = hidden_in.shape[0]
    pieces = (
        lax.all_gather(query_weight, "dp", axis=0, tiled=True),
        lax.all_gather(key_weight, "dp", axis=0, tiled=True),
        lax.all_gather(value_weight, "dp", axis=0, tiled=True),
    )
    query, keys, values = tuple(
        (jnp.dot(hidden_in, piece, preferred_element_type=jnp.float32) for piece in pieces)
    )
    head_size = key_weight.shape[1]
    heads_here = query.shape[1] // head_size
    positions = jnp.arange(tok, dtype=jnp.float32)
    q_rot = rotate(query.reshape(tok, heads_here, head_size), positions).astype(jnp.bfloat16)
    k_rot = rotate(keys.reshape(tok, 1, head_size), positions)[:, 0].astype(jnp.bfloat16)
    v_b = values.astype(jnp.bfloat16)
    scores = jnp.einsum(
        "qhd,kd->hqk", q_rot, k_rot, preferred_element_type=jnp.float32
    ) * head_size ** (-0.5)
    order = jnp.arange(tok, dtype=jnp.int32)
    segment = segment_ids[0]
    allowed = (order[:, None] >= order[None, :]) & (segment[:, None] == segment[None, :])
    scores = jnp.where(allowed[None], scores, -1e30)
    peak = jnp.max(scores, axis=-1, keepdims=True)
    weights = jnp.exp(scores - peak)
    probs = (weights / jnp.sum(weights, axis=-1, keepdims=True)).astype(jnp.bfloat16)
    context = jnp.einsum("hqk,kd->qhd", probs, v_b, preferred_element_type=jnp.float32)
    context = context.astype(jnp.bfloat16).reshape(tok, heads_here * head_size)
    full = lax.dot_general(
        context,
        lax.all_gather(output_weight, "dp", axis=0, tiled=True),
        (((1,), (1,)), ((), ())),
        preferred_element_type=jnp.float32,
    )
    n_dp = lax.axis_size("dp")
    n_head = lax.axis_size("head")
    shard_rows = full.shape[1] // (n_dp * n_head)
    shaped = full.reshape(tok, n_dp, n_head, shard_rows)
    mine = lax.psum_scatter(shaped, "head", scatter_dimension=2, tiled=True)
    return mine.reshape(tok, n_dp * shard_rows).astype(jnp.bfloat16)


def solution(mesh):
    placed = (
        P(None, ("dp", "head"), None),
        P(None, ("dp", "head"), None),
        P(None, ("dp", "head"), None),
        P(None, ("head", "dp"), None),
        P("dp", None),
        P("dp", None),
    )
    return jax.shard_map(
        shards, mesh=mesh, in_specs=placed, out_specs=P("dp", "head"), check_vma=False
    )
```

profile of v0, /device:TPU:1, one launch (start us, length us, event | category | flops | bytes accessed | tf_op | source)
XLA Modules:
  0.0 680.0 jit_solution(2034700656391935076)
XLA Ops:
  6.5 1.6 copy.64
  8.1 1.5 reshape.173
  9.7 6.8 %all-to-all-start.1 = ((bf16[16,2,8192]{2,1,0:T(2,128)(2,1)}), bf16[16,2,8192]{2,1,0:T(2,128)(2,1)S(1)}, u32[]{:S(2)}, u32[]{:S(2)}) async-start(bf16[16,2,8192]{2,1,0:T(2,128)(2,1)} %reshape.173), calls=%async_computation.1 | async-start | bytes 1048576 | tf_op jit(solution)/shard_map/all_to_all | solution.py:36
  16.5 12.7 %copy.67 = bf16[4,64,8192]{1,0,2:T(4,128)(2,1)} copy(bf16[4,64,8192]{2,1,0:T(8,128)(2,1)} %param.6) | data formatting | bytes 8388608 | tf_op args[0]
  29.2 14.0 %reshape.171 = bf16[16,2,65536]{2,1,0:T(2,128)(2,1)} reshape(bf16[8192,4,64]{2,1,0:T(4,128)(2,1)} %bitcast.80) | data formatting | bytes 8388608
  43.2 5.7 all-to-all-start.2
  49.0 0.7 reshape.174
  49.6 1.5 convert_reduce_fusion.2
  51.5 0.4 copy.66
  52.3 1.2 collective-permute-done.1
  53.5 0.8 maximum_select_fusion.1
  54.3 0.5 all-gather.9.cloned.1.call-start
  54.8 50.0 %all-to-all-done.2 = bf16[16,2,65536]{2,1,0:T(2,128)(2,1)} async-done(((bf16[16,2,65536]{2,1,0:T(2,128)(2,1)}), bf16[16,2,65536]{2,1,0:T(2,128)(2,1)}, u32[]{:S(2)}, u32[]{:S(2)}) %all-to-all-start.2) | async-done | bytes 4194336 | tf_op jit(solution)/shard_map/all_to_all | solution.py:35
  104.8 13.7 %reshape.172 = bf16[8192,4,64]{2,1,0:T(4,128)(2,1)} reshape(bf16[16,2,65536]{2,1,0:T(2,128)(2,1)} %all-to-all-done.2) | data formatting | bytes 8388608
  118.5 33.7 %convert_reduce_fusion.1 = f32[64,8192]{0,1:T(8,128)} fusion(bf16[8192,4,64]{2,1,0:T(4,128)(2,1)} %reshape.172), kind=kLoop, calls=%fused_computation.2 | loop fusion | flops 3670016 | bytes 6291456 | tf_op jit(solution)/shard_map/reduce_sum | solution.py:16
  152.2 2.8 copy.68
  155.2 0.4 copy.88
  155.6 1.6 copy.69
  157.2 0.7 copy.61
  157.9 1.5 reshape.175
  159.5 5.1 all-to-all-start
  164.6 12.9 %copy.74 = bf16[4,64,8192]{1,0,2:T(4,128)(2,1)} copy(bf16[4,64,8192]{2,1,0:T(8,128)(2,1)} %param.9) | data formatting | bytes 8388608 | tf_op args[3]
  177.4 14.0 %reshape.177 = bf16[16,2,65536]{2,1,0:T(2,128)(2,1)} reshape(bf16[8192,4,64]{2,1,0:T(4,128)(2,1)} %bitcast.81) | data formatting | bytes 8388608
  191.5 5.7 all-to-all-start.3
  197.2 0.7 reshape.176
  197.9 1.5 convert_reduce_fusion.3
  199.8 0.4 copy.63
  200.6 1.2 collective-permute-done
  201.8 0.8 maximum_select_fusion
  202.8 51.3 %all-to-all-done.3 = bf16[16,2,65536]{2,1,0:T(2,128)(2,1)} async-done(((bf16[16,2,65536]{2,1,0:T(2,128)(2,1)}), bf16[16,2,65536]{2,1,0:T(2,128)(2,1)}, u32[]{:S(2)}, u32[]{:S(2)}) %all-to-all-start.3) | async-done | bytes 4194336 | tf_op jit(solution)/shard_map/all_to_all | solution.py:38
  254.1 13.7 %reshape.178 = bf16[8192,4,64]{2,1,0:T(4,128)(2,1)} reshape(bf16[16,2,65536]{2,1,0:T(2,128)(2,1)} %all-to-all-done.3) | data formatting | bytes 8388608
  267.8 33.7 %convert_reduce_fusion = f32[64,8192]{0,1:T(8,128)} fusion(bf16[8192,4,64]{2,1,0:T(4,128)(2,1)} %reshape.178), kind=kLoop, calls=%fused_computation.1 | loop fusion | flops 3670016 | bytes 6291456 | tf_op jit(solution)/shard_map/reduce_sum | solution.py:16
  301.4 2.8 copy.75
  304.8 1.6 copy.76
  306.5 0.6 dynamic-slice
  307.3 1.0 fusion.14
  308.3 6.9 %convolution_bitcast_fusion = f32[512,1,128]{0,2,1:T(8,128)S(1)} fusion(bf16[8192,128]{0,1:T(8,128)(2,1)} %all-gather.7.cloned.1.call-done, bf16[512,8192]{1,0:T(8,128)(2,1)} %param.10), kind=kOutput, calls=%fused_computation.16 | convolution fusion | flops 1073741824 | bytes 10747904 | tf_op jit(solution)/shard_map/dot_general | solution.py:64
  315.3 0.6 subtract_convert_fusion.1
  315.9 10.0 %fusion.24 = f32[512,512]{1,0:T(8,128)S(1)} fusion(bf16[8192,512]{1,0:T(8,128)(2,1)} %all-gather.9.cloned.1.call-done, bf16[512,8192]{1,0:T(8,128)(2,1)} %param.10), kind=kOutput, calls=%fused_computation.49 | convolution fusion | flops 4294967296 | bytes 17825792 | tf_op jit(solution)/shard_map/dot_general | solution.py:64
  327.0 0.8 fusion.9
  327.8 4.0 fusion.23
  331.7 30.4 %all-gather.5.cloned.1.call-done = bf16[8192,128]{0,1:T(8,128)(2,1)} async-done(((bf16[1024,128]{0,1:T(8,128)(2,1)}), bf16[8192,128]{0,1:T(8,128)(2,1)}) %all-gather.5.cloned.1.call-update) | async-done | bytes 2097168 | tf_op jit(solution)/shard_map/all_gather | solution.py:61
  362.1 8.5 %fusion.6 = bf16[128,4,512]{2,0,1:T(8,128)(2,1)S(1)} fusion(f32[4,512,512]{1,2,0:T(8,128)} %get-tuple-element.14, f32[4,512]{1,0:T(4,128)S(1)} %get-tuple-element.13, bf16[8192,128]{0,1:T(8,128)(2,1)} %all-gather.5.cloned.1.call-done, bf16[512,8192]{1,0:T(8,128)(2,1)} %param.10), kind=kOutput, calls=%fused_computation.15 | convolution fusion | flops 1344602112 | bytes 15212544 | tf_op jit(solution)/shard_map/hqk,kd->qhd/dot_general | solution.py:82
  370.6 98.7 %all-gather.11.cloned.1.call-done = bf16[8192,512]{1,0:T(8,128)(2,1)} async-done(((bf16[1024,512]{1,0:T(8,128)(2,1)}), bf16[8192,512]{1,0:T(8,128)(2,1)}) %all-gather.11.cloned.1.call-update) | async-done | bytes 8388624 | tf_op jit(solution)/shard_map/all_gather | solution.py:86
  469.4 11.6 %fusion.25 = f32[512,8,16,64]{0,3,2,1:T(8,128)} fusion(bf16[512,512,1,1]{0,1,3,2:T(8,128)(2,1)S(1)} %bitcast.96, bf16[8,16,64,512]{3,2,1,0:T(8,128)(2,1)} %bitcast.95), kind=kOutput, calls=%fused_computation.50 | convolution fusion | flops 4294967296 | bytes 25690112 | tf_op jit(solution)/shard_map/dot_general | solution.py:84
  481.0 189.5 %all-reduce.2 = bf16[512,8,16,64]{0,3,2,1:T(8,128)(2,1)} all-reduce(f32[512,8,16,64]{0,3,2,1:T(8,128)} %fusion.25), channel_id=2, replica_groups=mesh['dp'=8,'head'=16] {'head'}, use_global_device_ids=true, to_apply=%region_6.7.clone | all-reduce | flops 4194304 | bytes 25165824
  670.5 1.7 dynamic-slice_convert_fusion
  672.2 1.0 copy.78
  (36 shorter events, 3.9 us)
Async XLA Ops:
  9.7 33.5 %all-to-all-start.1 = ((bf16[16,2,8192]{2,1,0:T(2,128)(2,1)}), bf16[16,2,8192]{2,1,0:T(2,128)(2,1)S(1)}, u32[]{:S(2)}, u32[]{:S(2)}) async-start(bf16[16,2,8192]{2,1,0:T(2,128)(2,1)} %reshape.173), calls=%async_computation.1 | async-start | bytes 1048576 | tf_op jit(solution)/shard_map/all_to_all | solution.py:36
  43.2 61.7 %all-to-all-start.2 = ((bf16[16,2,65536]{2,1,0:T(2,128)(2,1)}), bf16[16,2,65536]{2,1,0:T(2,128)(2,1)}, u32[]{:S(2)}, u32[]{:S(2)}) async-start(bf16[16,2,65536]{2,1,0:T(2,128)(2,1)} %reshape.171), calls=%async_computation.2 | async-start | bytes 8388608 | tf_op jit(solution)/shard_map/all_to_all | solution.py:35
  48.9 259.4 %all-gather.7.cloned.1.call-start = ((), (), s32[]{:S(2)}) async-start(), calls=%async_computation.5 | async-start | bytes 2359296 | tf_op jit(solution)/shard_map/all_gather | solution.py:60
  52.1 1.4 collective-permute-start.1
  54.3 261.6 %all-gather.9.cloned.1.call-start = ((), (), s32[]{:S(2)}) async-start(), calls=%async_computation.6 | async-start | bytes 9437184 | tf_op jit(solution)/shard_map/all_gather | solution.py:59
  155.1 2.1 copy-start
  159.5 32.0 %all-to-all-start = ((bf16[16,2,8192]{2,1,0:T(2,128)(2,1)}), bf16[16,2,8192]{2,1,0:T(2,128)(2,1)S(1)}, u32[]{:S(2)}, u32[]{:S(2)}) async-start(bf16[16,2,8192]{2,1,0:T(2,128)(2,1)} %reshape.175), calls=%async_computation | async-start | bytes 1048576 | tf_op jit(solution)/shard_map/all_to_all | solution.py:37
  191.5 62.6 %all-to-all-start.3 = ((bf16[16,2,65536]{2,1,0:T(2,128)(2,1)}), bf16[16,2,65536]{2,1,0:T(2,128)(2,1)}, u32[]{:S(2)}, u32[]{:S(2)}) async-start(bf16[16,2,65536]{2,1,0:T(2,128)(2,1)} %reshape.177), calls=%async_computation.3 | async-start | bytes 8388608 | tf_op jit(solution)/shard_map/all_to_all | solution.py:38
  197.2 165.0 %all-gather.5.cloned.1.call-start = ((), (), s32[]{:S(2)}) async-start(), calls=%async_computation.4 | async-start | bytes 2359296 | tf_op jit(solution)/shard_map/all_gather | solution.py:61
  200.4 1.4 collective-permute-start
  202.6 266.8 %all-gather.11.cloned.1.call-start = ((), (), s32[]{:S(2)}) async-start(), calls=%async_computation.7 | async-start | bytes 9437184 | tf_op jit(solution)/shard_map/all_gather | solution.py:86
  304.3 2.2 copy-start.2
  304.3 2.8 copy-start.1
Sparse Core Ops, SparseCore 0:
  54.4 72.9 all-gather.6
  157.3 150.4 all-gather.8
  310.2 51.9 all-gather.4
  364.3 104.9 all-gather.10
where the time goes:
time: 687 us; the launch traced here: 680 us
  waiting for transfers between devices  233 us (34%)
  blocking collectives  190 us (28%)
  local copies, waits for them, and re-layouts  103 us (15%)
  other arithmetic  78.1 us (11%)
  matrix products  37.9 us (6%)
  starting transfers between devices  24.6 us (4%)
  between operations  13.7 us (2%)
    unnamed x1, blocking collectives  190 us
    all_gather x1, waiting for transfers between devices, shards(): lax.all_gather(output_weight, 'dp', axis=0, tiled=True)  98.7 us
    unnamed x23, local copies, waits for them, and re-layouts  89.6 us
    reduce_sum x4, other arithmetic, average(): jnp.sum(stack.astype(jnp.float32), axis=0) * 0.25  70.3 us
    all_to_all x1, waiting for transfers between devices, shards(): lax.all_to_all(ckpt_output, 'head', split_axis=2, concat_axis=1, tiled=True)  51.3 us
    all_to_all x1, waiting for transfers between devices, shards(): lax.all_to_all(ckpt_query, 'head', split_axis=2, concat_axis=1, tiled=True)  50 us
    all_gather x1, waiting for transfers between devices, shards(): lax.all_gather(value_weight, 'dp', axis=0, tiled=True)  30.4 us
    dot_general x2, matrix products, shards(): jnp.dot(hidden_in, piece, preferred_element_type=jnp.float32)  17 us
  transfers between devices with their start and end apart: 10, of which 6 were waited for; matrix products, arithmetic and copies ran while one was open for 30% of the time, Pallas kernels for 0%

commit v1 on v0

v1 whole, which is shorter than its diff:
```python
import jax
import jax.numpy as jnp
from jax import lax
from jax.sharding import PartitionSpec as P

rope_base = 500000.0


def average(stack):
    return (jnp.sum(stack.astype(jnp.float32), axis=0) * 0.25).astype(jnp.bfloat16)


def rotate(values, positions):
    half = values.shape[-1] // 2
    freq = rope_base ** (-2.0 * jnp.arange(half, dtype=jnp.float32) / values.shape[-1])
    angle = positions[:, None] * freq[None, :]
    cosine = jnp.cos(angle)[:, None, :]
    sine = jnp.sin(angle)[:, None, :]
    first = values[..., :half]
    second = values[..., half:]
    return jnp.concatenate(
        [first * cosine - second * sine, second * cosine + first * sine], axis=-1
    )


def shards(ckpt_query, ckpt_key, ckpt_value, ckpt_output, hidden_in, segment_ids):
    n_dp = lax.axis_size("dp")
    n_head = lax.axis_size("head")
    rows, wide = ckpt_query.shape[1:]
    kv_wide = ckpt_key.shape[2]
    output_rows = lax.all_gather(average(ckpt_output), "dp", axis=0, tiled=True)
    mean_query = average(ckpt_query).reshape(rows, n_head, wide // n_head)
    mean_key = average(ckpt_key).reshape(rows, n_head, kv_wide // n_head)
    mean_value = average(ckpt_value).reshape(rows, n_head, kv_wide // n_head)
    packed = jnp.concatenate([mean_query, mean_key, mean_value], axis=2).transpose(1, 0, 2)
    moved = lax.all_to_all(packed, "head", split_axis=0, concat_axis=0, tiled=True)
    gathered = lax.all_gather(moved.reshape(n_head * rows, -1), "dp", axis=0, tiled=True)
    tok = hidden_in.shape[0]
    projected = jnp.dot(hidden_in, gathered, preferred_element_type=jnp.float32)
    query = projected[:, : wide // n_head]
    head_size = 2 * kv_wide // n_head
    own = projected[:, wide // n_head :]
    position = lax.axis_index("head")
    other = lax.ppermute(own, "head", [(i, i ^ 1) for i in range(n_head)])
    half = head_size // 2
    lower = position % 2 == 0
    low = jnp.where(lower, own, other)
    high = jnp.where(lower, other, own)
    keys = jnp.concatenate([low[:, :half], high[:, :half]], axis=1)
    values = jnp.concatenate([low[:, half:], high[:, half:]], axis=1)
    heads_here = query.shape[1] // head_size
    positions = jnp.arange(tok, dtype=jnp.float32)
    q_rot = rotate(query.reshape(tok, heads_here, head_size), positions).astype(jnp.bfloat16)
    k_rot = rotate(keys.reshape(tok, 1, head_size), positions)[:, 0].astype(jnp.bfloat16)
    v_b = values.astype(jnp.bfloat16)
    scores = jnp.einsum(
        "qhd,kd->hqk", q_rot, k_rot, preferred_element_type=jnp.float32
    ) * head_size ** (-0.5)
    order = jnp.arange(tok, dtype=jnp.int32)
    segment = segment_ids[0]
    allowed = (order[:, None] >= order[None, :]) & (segment[:, None] == segment[None, :])
    scores = jnp.where(allowed[None], scores, -1e30)
    peak = jnp.max(scores, axis=-1, keepdims=True)
    weights = jnp.exp(scores - peak)
    probs = (weights / jnp.sum(weights, axis=-1, keepdims=True)).astype(jnp.bfloat16)
    context = jnp.einsum("hqk,kd->qhd", probs, v_b, preferred_element_type=jnp.float32)
    context = context.astype(jnp.bfloat16).reshape(tok, heads_here * head_size)
    everyone = lax.all_gather(context, "head", axis=0)
    weight = output_rows.reshape(output_rows.shape[0], n_head, wide // n_head)
    result = lax.dot_general(
        everyone,
        weight,
        (((0, 2), (1, 2)), ((), ())),
        preferred_element_type=jnp.float32,
    )
    return result.astype(jnp.bfloat16)


def solution(mesh):
    placed = (
        P(None, ("dp", "head"), None),
        P(None, ("dp", "head"), None),
        P(None, ("dp", "head"), None),
        P(None, ("head", "dp"), None),
        P("dp", None),
        P("dp", None),
    )
    return jax.shard_map(
        shards, mesh=mesh, in_specs=placed, out_specs=P("dp", "head"), check_vma=False
    )
```

time: 687 us -> 343 us (0.50)
  blocking collectives: 190 us -> 25.1 us
  local copies, waits for them, and re-layouts: 103 us -> 15.7 us
  other arithmetic: 78.1 us -> 15.4 us
  starting transfers between devices: 24.6 us -> 1.43 us
  matrix products: 37.9 us -> 23.5 us
  waiting for transfers between devices: 233 us -> 247 us
    unnamed x1 -> x0, blocking collectives: 190 us -> none
    all_gather x4 -> x3, waiting for transfers between devices: 129 us -> 247 us  [the longest x1 120 us: shards(): lax.all_gather(moved.reshape(n_head * rows, -1), 'dp', axis=0, tiled=True)]
    all_to_all x4 -> x0, waiting for transfers between devices: 101 us -> none  [the longest x1 51.3 us: shards(): lax.all_to_all(ckpt_output, 'head', split_axis=2, concat_axis=1, tiled=True)]
    unnamed x23 -> x7, local copies, waits for them, and re-layouts: 89.6 us -> 1.03 us
    reduce_sum x4, other arithmetic: 70.3 us -> 8.62 us  [average(): jnp.sum(stack.astype(jnp.float32), axis=0) * 0.25]
    all_to_all x0 -> x1, blocking collectives: none -> 25.1 us  [shards(): lax.all_to_all(packed, 'head', split_axis=0, concat_axis=0, tiled=True)]
    all_to_all x4 -> x0, starting transfers between devices: 23.4 us -> none  [the longest x1 6.83 us: shards(): lax.all_to_all(ckpt_key, 'head', split_axis=2, concat_axis=1, tiled=True)]
    all_gather x0 -> x1, local copies, waits for them, and re-layouts: none -> 12 us  [shards(): output_rows = lax.all_gather(average(ckpt_output), 'dp', axis=0, tiled=True)]
  transfers between devices with their start and end apart: 10 -> 4, of which waited for: 6 -> 4; matrix products, arithmetic and copies ran while one was open for 30% -> 11% of each run, Pallas kernels for 0% -> 0%
where the time goes in v1:
time: 343 us; the launch traced here: 342 us
  waiting for transfers between devices  247 us (72%)
  blocking collectives  25.1 us (7%)
  matrix products  23.5 us (7%)
  local copies, waits for them, and re-layouts  15.7 us (5%)
  other arithmetic  15.4 us (4%)
  between operations  13.3 us (4%)
    all_gather x1, waiting for transfers between devices, shards(): lax.all_gather(moved.reshape(n_head * rows, -1), 'dp', axis=0, tiled=True)  120 us
    all_gather x1, waiting for transfers between devices, shards(): output_rows = lax.all_gather(average(ckpt_output), 'dp', axis=0, tiled=True)  86.2 us
    all_gather x1, waiting for transfers between devices, shards(): everyone = lax.all_gather(context, 'head', axis=0)  40.3 us
    all_to_all x1, blocking collectives, shards(): lax.all_to_all(packed, 'head', split_axis=0, concat_axis=0, tiled=True)  25.1 us
    all_gather x1, local copies, waits for them, and re-layouts, shards(): output_rows = lax.all_gather(average(ckpt_output), 'dp', axis=0, tiled=True)  12 us
    dot_general x1, matrix products, shards(): projected = jnp.dot(hidden_in, gathered, preferred_element_type=jnp.float32)  11.2 us
    dot_general x1, matrix products, shards(): lax.dot_general(everyone, weight, (((0, 2), (1, 2)), ((), ())), preferred...  11 us
    reduce_sum x4, other arithmetic, average(): jnp.sum(stack.astype(jnp.float32), axis=0) * 0.25  8.62 us
  transfers between devices with their start and end apart: 4, of which 4 were waited for; matrix products, arithmetic and copies ran while one was open for 11% of the time, Pallas kernels for 0%

profile of v1, /device:TPU:1, one launch (start us, length us, event | category | flops | bytes accessed | tf_op | source)
XLA Modules:
  0.0 342.0 jit_solution(17139786216191566086)
XLA Ops:
  6.5 0.0 all-gather.4.cloned.1.call-start
  6.5 1.1 convert_reduce_fusion.3
  7.7 0.2 convert_element_type.59
  7.9 1.2 convert_reduce_fusion.2
  9.1 0.2 convert_element_type.62
  9.3 3.2 convert_reduce_fusion.1
  12.4 0.1 multiply_convert_fusion.1
  12.6 0.4 copy.40
  12.9 0.2 maximum_bitcast_fusion
  13.1 0.3 copy.26
  13.4 25.1 %all_to_all.5 = bf16[16,64,640]{2,1,0:T(8,128)(2,1)} all-to-all(bf16[16,64,640]{2,1,0:T(8,128)(2,1)S(1)} %copy.26), channel_id=1, replica_groups=mesh['dp'=8,'head'=16] {'head'}, dimensions={0} | all-to-all | bytes 2621440 | tf_op jit(solution)/shard_map/all_to_all | solution.py:36
  38.6 0.0 all-gather.4.cloned.1.call-update
  38.6 0.0 copy-start.1
  38.6 0.0 all-gather.8.cloned.1.call-start
  38.6 3.2 convert_reduce_fusion
  41.8 1.2 multiply_convert_fusion
  43.0 0.0 all-gather.8.cloned.1.call-update
  43.0 0.0 all-gather.6.cloned.1.call-start
  43.1 0.0 copy-done.1
  43.1 0.2 fusion.8
  43.3 1.0 fusion.14
  44.3 120.4 %all-gather.4.cloned.1.call-done = bf16[8192,640]{1,0:T(8,128)(2,1)} async-done(((bf16[1024,640]{1,0:T(8,128)(2,1)}), bf16[8192,640]{1,0:T(8,128)(2,1)}) %all-gather.4.cloned.1.call-update) | async-done | bytes 10485776 | tf_op jit(solution)/shard_map/all_gather | solution.py:37
  164.6 11.2 %convolution_bitcast_fusion = f32[512,640]{0,1:T(8,128)S(1)} fusion(bf16[8192,640]{1,0:T(8,128)(2,1)} %all-gather.4.cloned.1.call-done, bf16[512,8192]{1,0:T(8,128)(2,1)} %param.10), kind=kOutput, calls=%fused_computation.13 | convolution fusion | flops 5368709120 | bytes 20185088 | tf_op jit(solution)/shard_map/dot_general | solution.py:39
  175.9 0.0 copy-start
  175.9 0.8 slice.42
  176.7 0.1 slice.49
  176.8 1.3 collective-permute-start
  178.1 0.1 fusion.25
  178.2 0.0 copy-done
  178.2 0.3 copy.39
  178.6 0.3 copy.38
  178.9 0.3 subtract_convert_fusion
  179.2 0.4 collective-permute-done
  179.6 1.1 broadcast_select_fusion.1
  180.8 0.6 subtract_convert_fusion.1
  181.4 0.8 fusion.9
  182.1 2.1 fusion.26
  184.3 0.5 fusion.6
  184.8 1.0 copy.31
  185.8 0.0 all-gather.6.cloned.1.call-update
  185.8 86.2 %all-gather.8.cloned.1.call-done = bf16[512,8192]{1,0:T(8,128)(2,1)} async-done(((bf16[64,8192]{1,0:T(8,128)(2,1)}), bf16[512,8192]{1,0:T(8,128)(2,1)}) %all-gather.8.cloned.1.call-update) | async-done | bytes 8388624 | tf_op jit(solution)/shard_map/all_gather | solution.py:31
  272.0 12.0 %copy.32 = bf16[512,8192]{0,1:T(8,128)(2,1)} copy(bf16[512,8192]{1,0:T(8,128)(2,1)} %all-gather.8.cloned.1.call-done) | data formatting | bytes 16777216 | tf_op jit(solution)/shard_map/all_gather | solution.py:31
  284.1 40.3 %all-gather.6.cloned.1.call-done = bf16[16,512,512]{2,1,0:T(8,128)(2,1)} async-done(((bf16[1,512,512]{2,1,0:T(8,128)(2,1)}), bf16[16,512,512]{2,1,0:T(8,128)(2,1)}) %all-gather.6.cloned.1.call-update) | async-done | bytes 8388624 | tf_op jit(solution)/shard_map/all_gather | solution.py:68
  324.4 11.0 %fusion.7 = bf16[512,512]{1,0:T(8,128)(2,1)} fusion(bf16[16,512,512]{2,1,0:T(8,128)(2,1)} %all-gather.6.cloned.1.call-done, bf16[512,16,512]{0,2,1:T(8,128)(2,1)} %bitcast.42), kind=kOutput, calls=%fused_computation.17 | convolution fusion | flops 4295229440 | bytes 17301504 | tf_op jit(solution)/shard_map/dot_general | solution.py:70
  (8 shorter events, 0.1 us)
Async XLA Ops:
  6.5 158.1 %all-gather.4.cloned.1.call-start = ((), (), s32[]{:S(2)}) async-start(), calls=%async_computation.1 | async-start | bytes 11796480 | tf_op jit(solution)/shard_map/all_gather | solution.py:37
  38.6 4.5 %copy-start.1 = (s32[1,512]{1,0:T(1,128)S(1)}, s32[1,512]{1,0:T(1,128)}, u32[]{:S(2)}) copy-start(s32[1,512]{1,0:T(1,128)} %param.11) | copy-start | bytes 6148
  38.6 233.4 %all-gather.8.cloned.1.call-start = ((), (), s32[]{:S(2)}) async-start(), calls=%async_computation.3 | async-start | bytes 9437184 | tf_op jit(solution)/shard_map/all_gather | solution.py:31
  43.0 281.4 %all-gather.6.cloned.1.call-start = ((), (), s32[]{:S(2)}) async-start(), calls=%async_computation.2 | async-start | bytes 8912896 | tf_op jit(solution)/shard_map/all_gather | solution.py:68
  175.9 2.3 copy-start
  176.8 2.8 collective-permute-start
Sparse Core Ops, SparseCore 0:
  38.7 125.9 all-gather.3
  167.0 104.9 all-gather.7
  273.7 50.6 all-gather.5

commit v2 on v1

v2 whole, which is shorter than its diff:
```python
import functools

import jax
import jax.numpy as jnp
import numpy as np
from jax import lax
from jax.experimental import pallas as pl
from jax.experimental.pallas import tpu as pltpu
from jax.sharding import PartitionSpec as P

MESH = pl.DeviceIdType.MESH
rope_base = 500000.0
N = 4
TOK = 512
HEAD = 128
HEADS_CHIP = 4
QCOLS = HEADS_CHIP * HEAD
WCOLS = QCOLS + HEAD
ROWS = 64
D = 8192
SUB = 4
PIECE = D // N


def average(stack):
    return (jnp.sum(stack.astype(jnp.float32), axis=0) * 0.25).astype(jnp.bfloat16)


def wrap(value):
    return lax.rem(value, N)


def device(x, y, z, c):
    return (2 * z + lax.div(y, 2), 8 * lax.rem(y, 2) + 2 * x + c)


def kernel(
    ckpt_q, ckpt_k, ckpt_v, ckpt_o, hidden, segments, cosine, sine, out,
    stage_q, stage_kv, stage_o, mean_kv, send_w, send_o, weights, hid, acc, weights_o,
    ctx, q_rot, kv, seg, table, out_block,
    stage_q_sem, stage_sem, a2a_send, a2a_recv, z_send, z_recv, pair_send, pair_recv,
    hid_sem, cross_send, cross_recv, ring_send, ring_recv, kv_sem, seg_sem,
    swap_sem, zo_send, zo_recv, pair_o_send, pair_o_recv, ctx_send, ctx_recv, out_sem,
):
    dp = lax.axis_index("dp")
    head = lax.axis_index("head")
    z = lax.div(dp, 2)
    y_hi = lax.rem(dp, 2)
    y = 2 * y_hi + lax.div(head, 8)
    x = wrap(lax.div(head, 2))
    c = lax.rem(head, 2)
    place = 4 * y + x
    owner = c == y_hi
    up, down, far = wrap(z + 1), wrap(z + 3), wrap(z + 2)
    here_up, here_down = device(x, y, up, c), device(x, y, down, c)
    partner = device(x, y, z, 1 - c)
    across = device(x, wrap(y + 2), z, 1 - c)
    cross = device(x, 3 - y, z, c)

    def remote(src, dst, send, recv, where):
        return pltpu.make_async_remote_copy(
            src_ref=src, dst_ref=dst, send_sem=send, recv_sem=recv,
            device_id=where, device_id_type=MESH,
        )

    def spot(k):
        dx, dy = lax.rem(k, N), lax.div(k, N)
        tx, ty = wrap(x + dx), wrap(y + dy)
        fx, fy = wrap(x + N - dx), wrap(y + N - dy)
        return tx, ty, 4 * ty + tx, 4 * fy + fx

    def stage_copy(k):
        _, _, to, _ = spot(k)
        return pltpu.make_async_copy(
            ckpt_q.at[:, :, pl.ds(pl.multiple_of(to * QCOLS, QCOLS), QCOLS)],
            stage_q.at[k], stage_q_sem.at[k],
        )

    load_k = pltpu.make_async_copy(ckpt_k, stage_kv.at[0], stage_sem.at[0])
    load_v = pltpu.make_async_copy(ckpt_v, stage_kv.at[1], stage_sem.at[1])
    load_o = pltpu.make_async_copy(ckpt_o, stage_o, stage_sem.at[2])
    load_cos = pltpu.make_async_copy(cosine, table.at[0], stage_sem.at[3])
    load_sin = pltpu.make_async_copy(sine, table.at[1], stage_sem.at[4])
    load_k.start()
    load_v.start()

    @pl.loop(0, 16)
    def _(k):
        stage_copy(k).start()

    load_o.start()
    load_cos.start()
    load_sin.start()

    barrier = pltpu.get_barrier_semaphore()

    @pl.loop(1, 16)
    def _(k):
        tx, ty, _, _ = spot(k)
        pl.semaphore_signal(barrier, inc=1, device_id=device(tx, ty, z, c), device_id_type=MESH)

    for peer in (here_up, here_down, partner, across):
        pl.semaphore_signal(barrier, inc=1, device_id=peer, device_id_type=MESH)

    load_k.wait()
    load_v.wait()
    for which in range(2):
        for g in range(8):
            mean_kv[which, g] = average(stage_kv[which, :, :, g * HEAD : (g + 1) * HEAD])

    pl.semaphore_wait(barrier, 19)

    def a2a_copy(k):
        tx, ty, _, _ = spot(k)
        return remote(
            send_w.at[k], weights.at[z, place, c], a2a_send, a2a_recv.at[k], device(tx, ty, z, c)
        )

    def piece(k):
        _, _, to, _ = spot(k)
        stage_copy(k).wait()
        return average(stage_q[k]), mean_kv[lax.rem(to, 2), lax.div(to, 2)]

    first_q, first_kv = piece(0)
    weights[z, place, c, :, :QCOLS] = first_q
    weights[z, place, c, :, QCOLS:] = first_kv

    @pl.loop(1, 16)
    def _(k):
        mean_q, mean_pair = piece(k)
        send_w[k, :, :QCOLS] = mean_q
        send_w[k, :, QCOLS:] = mean_pair

        @pl.when(k > 1)
        def _():
            a2a_copy(k - 1).start()

    sub_rows = TOK // SUB

    def hid_part(ref, at_x, j):
        return ref.at[
            pl.ds(j * sub_rows, sub_rows), pl.ds(pl.multiple_of(at_x * PIECE, PIECE), PIECE)
        ]

    def cross_copy(j):
        return remote(
            hid_part(hidden, x, j), hid_part(hid, x, j), cross_send, cross_recv.at[j], cross
        )

    def seg_copy():
        return remote(segments, seg, seg_sem.at[0], seg_sem.at[1], cross)

    local_hid = pltpu.make_async_copy(hidden, hid, hid_sem.at[0])
    local_seg = pltpu.make_async_copy(segments, seg, hid_sem.at[1])

    a2a_copy(15).start()

    @pl.when(owner)
    def _():
        @pl.loop(0, SUB)
        def _(j):
            cross_copy(j).start()

        seg_copy().start()
        local_hid.start()
        local_seg.start()

    load_o.wait()
    step = D // 8

    @pl.when(owner)
    def _():
        @pl.loop(0, 8)
        def _(j):
            cols = pl.ds(pl.multiple_of(j * step, step), step)
            weights_o[z, c, :, cols] = average(stage_o[:, :, cols])

    def swap_copy():
        return remote(
            send_o, weights_o.at[z, y_hi], swap_sem.at[0], swap_sem.at[1], across
        )

    @pl.when(jnp.logical_not(owner))
    def _():
        @pl.loop(0, 8)
        def _(j):
            cols = pl.ds(pl.multiple_of(j * step, step), step)
            send_o[:, cols] = average(stage_o[:, :, cols])

    def z_copy(level, k, direction, send_index, recv_index):
        _, _, _, source = spot(k)
        block = weights.at[level, source, c]
        return remote(
            block, block, z_send.at[send_index], z_recv.at[recv_index, k],
            here_up if direction > 0 else here_down,
        )

    def pair_copy(level, k, slot):
        _, _, _, source = spot(k)
        block = weights.at[level, source, c]
        return remote(block, block, pair_send, pair_recv.at[slot], partner)

    def pair_done(level, slot):
        block = weights.at[level, :, 1 - c]
        return remote(block, block, pair_send, pair_recv.at[slot], partner)

    def a2a_arrival(k):
        _, _, _, source = spot(k)
        block = weights.at[z, source, c]
        return remote(block, block, a2a_send, a2a_recv.at[k], partner)

    @pl.loop(0, 16)
    def _(k):
        @pl.when(k > 0)
        def _():
            a2a_arrival(k).wait_recv()

        z_copy(z, k, 1, 0, 0).start()
        z_copy(z, k, -1, 1, 1).start()
        pair_copy(z, k, 0).start()

    @pl.when(jnp.logical_not(owner))
    def _():
        swap_copy().start()

    def ring_copy(at_x, j, direction, slot):
        block = hid_part(hid, at_x, j)
        to = wrap(x + direction)
        return remote(block, block, ring_send, ring_recv.at[slot, j], device(to, y, z, c))

    east, west, far_x = wrap(x + 1), wrap(x + 3), wrap(x + 2)

    @pl.loop(0, SUB)
    def _(j):
        @pl.when(jnp.logical_not(owner))
        def _():
            cross_copy(j).wait_recv()
            ring_copy(x, j, 1, 0).start()
            ring_copy(x, j, 3, 1).start()

        @pl.loop(0, 4)
        def _(i):
            k = 4 * j + i
            z_copy(down, k, 1, 0, 0).wait_recv()

            @pl.when(lax.rem(i, 2) == 0)
            def _():
                z_copy(down, k, 1, 0, 2).start()

            pair_copy(down, k, 1).start()
            z_copy(up, k, -1, 1, 1).wait_recv()

            @pl.when(lax.rem(i, 2) == 1)
            def _():
                z_copy(up, k, -1, 1, 2).start()

            pair_copy(up, k, 2).start()

    @pl.when(jnp.logical_not(owner))
    def _():
        @pl.loop(0, SUB)
        def _(j):
            ring_copy(west, j, 1, 0).wait_recv()

            @pl.when(lax.rem(j, 2) == 0)
            def _():
                ring_copy(west, j, 1, 2).start()

            ring_copy(east, j, 3, 1).wait_recv()

            @pl.when(lax.rem(j, 2) == 1)
            def _():
                ring_copy(east, j, 3, 2).start()

    def o_block(level, core, j):
        return weights_o.at[level, core, :, pl.ds(pl.multiple_of(j * PIECE, PIECE), PIECE)]

    def zo_copy(level, j, direction, send_index, recv_index):
        block = o_block(level, c, j)
        return remote(
            block, block, zo_send.at[send_index], zo_recv.at[recv_index, j],
            here_up if direction > 0 else here_down,
        )

    def pair_o_copy(level, j, slot):
        block = o_block(level, c, j)
        return remote(block, block, pair_o_send, pair_o_recv.at[slot], partner)

    def pair_o_done(level, slot):
        block = weights_o.at[level, 1 - c]
        return remote(block, block, pair_o_send, pair_o_recv.at[slot], partner)

    @pl.when(jnp.logical_not(owner))
    def _():
        block = weights_o.at[z, c]
        remote(block, block, swap_sem.at[0], swap_sem.at[1], across).wait_recv()

    @pl.loop(0, SUB)
    def _(j):
        zo_copy(z, j, 1, 0, 0).start()
        zo_copy(z, j, -1, 1, 1).start()
        pair_o_copy(z, j, 0).start()

    @pl.loop(0, 16)
    def _(k):
        z_copy(far, k, 1, 0, 2).wait_recv()
        pair_copy(far, k, 3).start()

    @pl.when(owner)
    def _():
        local_hid.wait()
        local_seg.wait()

    @pl.when(jnp.logical_not(owner))
    def _():
        @pl.loop(0, SUB)
        def _(j):
            ring_copy(far_x, j, 1, 2).wait_recv()

        seg_copy().wait_recv()

    pair_done(z, 0).wait_recv()
    pair_done(down, 1).wait_recv()
    pair_done(up, 2).wait_recv()
    pair_done(far, 3).wait_recv()

    load_cos.wait()
    load_sin.wait()
    acc[...] = jnp.zeros_like(acc)

    def project(t, lo, hi):
        level, inner = lax.div(t, 2), lax.rem(t, 2)
        block = weights[level, pl.ds(8 * inner, 8), :, :, lo:hi].reshape(1024, hi - lo)
        rows = hid[:, pl.ds(pl.multiple_of(t * 1024, 1024), 1024)]
        acc[:, lo:hi] += jnp.dot(rows, block, preferred_element_type=jnp.float32)

    def rotate(values):
        return values * table[0] + pltpu.roll(values, HEAD // 2, 1) * table[1]

    @pl.loop(0, 8)
    def _(t):
        project(t, QCOLS, WCOLS)

    parity = lax.rem(x, 2)
    mine = acc[:, QCOLS:]
    kv[parity] = jnp.where(parity == 0, rotate(mine), mine).astype(jnp.bfloat16)

    @pl.loop(0, 8)
    def _(t):
        project(t, 0, QCOLS)

    kv_peer = device(x + 1 - 2 * parity, y, z, c)
    kv_out = remote(kv.at[parity], kv.at[parity], kv_sem.at[0], kv_sem.at[1], kv_peer)
    kv_in = remote(kv.at[1 - parity], kv.at[1 - parity], kv_sem.at[0], kv_sem.at[1], kv_peer)
    kv_out.start()
    for h in range(HEADS_CHIP):
        q_rot[h] = rotate(acc[:, h * HEAD : (h + 1) * HEAD]).astype(jnp.bfloat16)
    kv_in.wait_recv()

    segment_row = seg[...].astype(jnp.float32)
    segment_col = jnp.transpose(jnp.broadcast_to(segment_row, (HEAD, TOK)))[:, :1]
    half = TOK // 2

    def ctx_copy(place_from, h, where, slot):
        block = ctx.at[place_from, h]
        return remote(block, block, ctx_send, ctx_recv.at[slot, h], where)

    def line(h, along, by):
        on_x = lax.rem(lax.div(h, 2) + along, 2) == 0
        step_x = jnp.where(on_x, by, 0)
        step_y = jnp.where(on_x, 0, by)
        return device(wrap(x + step_x), wrap(y + step_y), z, c)

    def block_at(h, first, second):
        on_x = lax.div(h, 2) == 0
        step_x = jnp.where(on_x, first, second)
        step_y = jnp.where(on_x, second, first)
        return 4 * wrap(y + step_y) + wrap(x + step_x)

    @pl.loop(0, HEADS_CHIP)
    def _(h):
        for part in range(2):
            rows = slice(part * half, (part + 1) * half)
            width = (part + 1) * half
            scores = lax.dot_general(
                q_rot[h, rows], kv[0, :width], (((1,), (1,)), ((), ())),
                preferred_element_type=jnp.float32,
            ) * HEAD ** (-0.5)
            row_at = lax.broadcasted_iota(jnp.int32, (half, width), 0) + part * half
            col_at = lax.broadcasted_iota(jnp.int32, (half, width), 1)
            allowed = (row_at >= col_at) & (segment_col[rows] == segment_row[:, :width])
            scores = jnp.where(allowed, scores, -1e30)
            peak = jnp.max(scores, axis=-1, keepdims=True)
            raised = jnp.exp(scores - peak)
            probs = (raised * (1.0 / jnp.sum(raised, axis=-1, keepdims=True))).astype(jnp.bfloat16)
            ctx[place, h, rows] = jnp.dot(
                probs, kv[1, :width], preferred_element_type=jnp.float32
            ).astype(jnp.bfloat16)

    @pl.loop(0, HEADS_CHIP)
    def _(h):
        ctx_copy(place, h, line(h, 0, 1), 1).start()
        ctx_copy(place, h, line(h, 0, 3), 3).start()
        ctx_copy(place, h, line(h, 1, 1), 4).start()
        ctx_copy(place, h, line(h, 1, 3), 12).start()

    @pl.loop(0, SUB)
    def _(j):
        zo_copy(down, j, 1, 0, 0).wait_recv()

        @pl.when(lax.rem(j, 2) == 0)
        def _():
            zo_copy(down, j, 1, 0, 2).start()

        pair_o_copy(down, j, 1).start()
        zo_copy(up, j, -1, 1, 1).wait_recv()

        @pl.when(lax.rem(j, 2) == 1)
        def _():
            zo_copy(up, j, -1, 1, 2).start()

        pair_o_copy(up, j, 2).start()

    def ctx_wait(h, first, second, slot):
        block = ctx.at[block_at(h, first, second), h]
        remote(block, block, ctx_send, ctx_recv.at[slot, h], partner).wait_recv()

    def onward(h, slot):
        even = lax.rem(h, 2) == 0
        source = block_at(h, 3 if slot == 1 else 1, 0)

        @pl.when(even if slot == 1 else jnp.logical_not(even))
        def _():
            ctx_copy(source, h, line(h, 0, slot), 2).start()

        ctx_copy(source, h, line(h, 1, 1), 4 + slot).start()
        ctx_copy(source, h, line(h, 1, 3), 12 + slot).start()

    @pl.loop(0, HEADS_CHIP)
    def _(h):
        ctx_wait(h, 3, 0, 1)
        onward(h, 1)
        ctx_wait(h, 1, 0, 3)
        onward(h, 3)

    @pl.loop(0, HEADS_CHIP)
    def _(h):
        ctx_wait(h, 2, 0, 2)
        source = block_at(h, 2, 0)
        ctx_copy(source, h, line(h, 1, 1), 4 + 2).start()
        ctx_copy(source, h, line(h, 1, 3), 12 + 2).start()

    @pl.loop(0, 4)
    def _(i):
        t = jnp.where(i == 2, 3, jnp.where(i == 3, 2, i))
        first = wrap(N - t)

        @pl.loop(0, HEADS_CHIP)
        def _(h):
            even = lax.rem(h, 2) == 0
            ctx_wait(h, first, 3, 4 + t)

            @pl.when(even)
            def _():
                ctx_copy(block_at(h, first, 3), h, line(h, 1, 1), 8 + t).start()

            ctx_wait(h, first, 1, 12 + t)

            @pl.when(jnp.logical_not(even))
            def _():
                ctx_copy(block_at(h, first, 1), h, line(h, 1, 3), 8 + t).start()

    @pl.loop(0, SUB)
    def _(j):
        zo_copy(far, j, 1, 0, 2).wait_recv()
        pair_o_copy(far, j, 3).start()

    @pl.loop(0, 4)
    def _(t):
        @pl.loop(0, HEADS_CHIP)
        def _(h):
            ctx_wait(h, wrap(N - t), 2, 8 + t)

    pair_o_done(z, 0).wait_recv()
    pair_o_done(down, 1).wait_recv()
    pair_o_done(up, 2).wait_recv()
    pair_o_done(far, 3).wait_recv()

    acc[:, :QCOLS] = jnp.zeros((TOK, QCOLS), jnp.float32)

    @pl.loop(0, 16)
    def _(p):
        rows = jnp.concatenate([ctx[p, h] for h in range(HEADS_CHIP)], axis=1)
        cols = weights_o[:, :, :, pl.ds(pl.multiple_of(p * QCOLS, QCOLS), QCOLS)]
        acc[:, :QCOLS] += lax.dot_general(
            rows, cols.reshape(TOK, QCOLS), (((1,), (1,)), ((), ())),
            preferred_element_type=jnp.float32,
        )

    out_block[...] = acc[:, :QCOLS].astype(jnp.bfloat16)

    @pl.when(owner)
    def _():
        stay = pltpu.make_async_copy(out_block, out, out_sem.at[2])
        stay.start()
        stay.wait()

    @pl.when(jnp.logical_not(owner))
    def _():
        leave = remote(out_block, out, out_sem.at[0], out_sem.at[1], across)
        leave.start()
        leave.wait()

    def drained(ref, sem):
        remote(ref, ref, sem, kv_sem.at[1], partner).wait_send()

    drained(weights.at[0, pl.ds(0, 15), 0], a2a_send)
    for direction in range(2):
        drained(weights.at[0, pl.ds(0, 12)], z_send.at[direction])
        drained(weights_o.at[pl.ds(0, 3), 0, :, pl.ds(0, 2 * PIECE)], zo_send.at[direction])
    drained(weights.at[:, :, 0], pair_send)
    drained(weights_o.at[:, 0], pair_o_send)
    drained(kv.at[0], kv_sem.at[0])
    drained(ctx.at[pl.ds(0, 15)], ctx_send)

    @pl.when(owner)
    def _():
        drained(hid.at[:, pl.ds(0, PIECE)], cross_send)
        drained(seg, seg_sem.at[0])

    @pl.when(jnp.logical_not(owner))
    def _():
        drained(hid.at[:, pl.ds(0, 3 * PIECE)], ring_send)
        drained(send_o, swap_sem.at[0])


def tables():
    half = HEAD // 2
    freq = np.float32(rope_base) ** (
        np.float32(-2.0) * np.arange(half, dtype=np.float32) / np.float32(HEAD)
    )
    angle = np.arange(TOK, dtype=np.float32)[:, None] * freq.astype(np.float32)[None, :]
    cosine, sine = np.cos(angle), np.sin(angle)
    return (
        np.concatenate([cosine, cosine], axis=1).astype(np.float32),
        np.concatenate([-sine, sine], axis=1).astype(np.float32),
    )


def shards(ckpt_query, ckpt_key, ckpt_value, ckpt_output, hidden_in, segment_ids):
    bf16, f32 = jnp.bfloat16, jnp.float32
    dma = pltpu.SemaphoreType.DMA
    cosine, sine = tables()
    anywhere = pl.BlockSpec(memory_space=pl.ANY)
    return pl.pallas_call(
        kernel,
        out_shape=jax.ShapeDtypeStruct((TOK, TOK), bf16),
        in_specs=[anywhere] * 8,
        out_specs=anywhere,
        scratch_shapes=[
            pltpu.VMEM((16, 4, ROWS, QCOLS), bf16),
            pltpu.VMEM((2, 4, ROWS, 1024), bf16),
            pltpu.VMEM((4, ROWS, D), bf16),
            pltpu.VMEM((2, 8, ROWS, HEAD), bf16),
            pltpu.VMEM((16, ROWS, WCOLS), bf16),
            pltpu.VMEM((ROWS, D), bf16),
            pltpu.VMEM((4, 16, 2, ROWS, WCOLS), bf16),
            pltpu.VMEM((TOK, D), bf16),
            pltpu.VMEM((TOK, WCOLS), f32),
            pltpu.VMEM((4, 2, ROWS, D), bf16),
            pltpu.VMEM((16, HEADS_CHIP, TOK, HEAD), bf16),
            pltpu.VMEM((HEADS_CHIP, TOK, HEAD), bf16),
            pltpu.VMEM((2, TOK, HEAD), bf16),
            pltpu.VMEM((1, TOK), jnp.int32),
            pltpu.VMEM((2, TOK, HEAD), f32),
            pltpu.VMEM((TOK, TOK), bf16),
            dma((16,)),
            dma((5,)),
            dma,
            dma((16,)),
            dma((2,)),
            dma((3, 16)),
            dma,
            dma((4,)),
            dma((2,)),
            dma,
            dma((SUB,)),
            dma,
            dma((3, SUB)),
            dma((2,)),
            dma((2,)),
            dma((2,)),
            dma((2,)),
            dma((3, SUB)),
            dma,
            dma((4,)),
            dma,
            dma((16, HEADS_CHIP)),
            dma((3,)),
        ],
        compiler_params=pltpu.CompilerParams(
            collective_id=0, has_side_effects=True, vmem_limit_bytes=66_000_000
        ),
    )(ckpt_query, ckpt_key, ckpt_value, ckpt_output, hidden_in, segment_ids, cosine, sine)


def solution(mesh):
    placed = (
        P(None, ("dp", "head"), None),
        P(None, ("dp", "head"), None),
        P(None, ("dp", "head"), None),
        P(None, ("head", "dp"), None),
        P("dp", None),
        P("dp", None),
    )
    return jax.shard_map(
        shards, mesh=mesh, in_specs=placed, out_specs=P("dp", "head"), check_vma=False
    )
```

time: 343 us -> 154 us (0.45)
  waiting for transfers between devices: 247 us -> 0 us
  Pallas kernels: 0 us -> 150 us
  blocking collectives: 25.1 us -> 0 us
  matrix products: 23.5 us -> 0 us
  other arithmetic: 15.4 us -> 0 us
  local copies, waits for them, and re-layouts: 15.7 us -> 1.87 us
  between operations: 13.3 us -> 0.01 us
    all_gather x3 -> x0, waiting for transfers between devices: 247 us -> none  [the longest x1 120 us: shards(): lax.all_gather(moved.reshape(n_head * rows, -1), 'dp', axis=0, tiled=True)]
    pallas_call x0 -> x1, Pallas kernels: none -> 150 us  [shards(): pl.pallas_call(kernel, out_shape=jax.ShapeDtypeStruct((TOK, TOK), bf16),...]
    all_to_all x1 -> x0, blocking collectives: 25.1 us -> none  [shards(): lax.all_to_all(packed, 'head', split_axis=0, concat_axis=0, tiled=True)]
    dot_general x4 -> x0, matrix products: 23.5 us -> none  [the longest x1 11.2 us: shards(): projected = jnp.dot(hidden_in, gathered, preferred_element_type=jnp.float32)]
    all_gather x1 -> x0, local copies, waits for them, and re-layouts: 12 us -> none  [shards(): output_rows = lax.all_gather(average(ckpt_output), 'dp', axis=0, tiled=True)]
    reduce_sum x4 -> x0, other arithmetic: 8.62 us -> none  [average(): jnp.sum(stack.astype(jnp.float32), axis=0) * 0.25]
  transfers between devices with their start and end apart: 4 -> 0, of which waited for: 4 -> 0; matrix products, arithmetic and copies ran while one was open for 11% -> 0% of each run, Pallas kernels for 0% -> 0%
where the time goes in v2:
time: 154 us; the launch traced here: 152 us
  Pallas kernels  150 us (97%)
  local copies, waits for them, and re-layouts  1.87 us (1%)
    pallas_call x1, Pallas kernels, shards(): pl.pallas_call(kernel, out_shape=jax.ShapeDtypeStruct((TOK, TOK), bf16),...  150 us

profile of v2, /device:TPU:1, one launch (start us, length us, event | category | flops | bytes accessed | tf_op | source)
XLA Modules:
  0.0 152.0 jit_solution(10068201414218009416)
XLA Ops:
  0.0 150.2 %shard_map.82 = bf16[512,512]{1,0:T(8,128)(2,1)} custom-call(bf16[4,64,8192]{2,1,0:T(8,128)(2,1)} %ckpt_q.1, bf16[4,64,1024]{2,1,0:T(8,128)(2,1)} %ckpt_k.1, bf16[4,64,1024]{2,1,0:T(8,128)(2,1)} %ckpt_v.1, bf16[4,64,8192]{2,1,0:T(8,128)(2,1)} %ckpt_o.1, bf16[512,8192]{1,0:T(8,128)(2,1)} %hidden.1, s32[1,512]{1,0:T(1,128)} %segments.1, ...), custom_call_target="tpu_custom_call" | custom-call | tf_op jit(solution)/shard_map/pallas_call | solution.py:555
  150.2 1.9 %copy.10 = bf16[512,512]{1,0:T(8,128)(2,1)} copy(bf16[512,512]{1,0:T(8,128)(2,1)} %shard_map.82) | data formatting | bytes 1048576

commit v3 on v2

v3 whole, which is shorter than its diff:
```python
import functools

import jax
import jax.numpy as jnp
import numpy as np
from jax import lax
from jax.experimental import pallas as pl
from jax.experimental.pallas import tpu as pltpu
from jax.sharding import PartitionSpec as P

MESH = pl.DeviceIdType.MESH
rope_base = 500000.0
N = 4
TOK = 512
HEAD = 128
HEADS_CHIP = 4
QCOLS = HEADS_CHIP * HEAD
WCOLS = QCOLS + HEAD
ROWS = 64
D = 8192
SUB = 4
PIECE = D // N
SUB_ROWS = TOK // 4
HALF = TOK // 2


def average(stack):
    return (jnp.sum(stack.astype(jnp.float32), axis=0) * 0.25).astype(jnp.bfloat16)


def wrap(value):
    return lax.rem(value, N)


def device(x, y, z, c):
    return (2 * z + lax.div(y, 2), 8 * lax.rem(y, 2) + 2 * x + c)


def kernel(
    ckpt_q, ckpt_k, ckpt_v, ckpt_o, hidden, segments, cosine, sine, out,
    stage_q, stage_kv, stage_o, mean_kv, send_w, send_o, weights, hid, acc, weights_o,
    ctx, q_rot, kv, seg, table, out_block,
    stage_q_sem, stage_sem, a2a_send, a2a_recv, z_send, z_recv, pair_send, pair_recv,
    hid_sem, cross_send, cross_recv, inner_send, inner_recv, ring_send, ring_recv, kv_sem, seg_sem,
    swap_sem, zo_send, zo_recv, pair_o_send, pair_o_recv, ctx_send, ctx_recv,
    stay_sem, leave_send, leave_recv,
):
    dp = lax.axis_index("dp")
    head = lax.axis_index("head")
    z = lax.div(dp, 2)
    y_hi = lax.rem(dp, 2)
    y = 2 * y_hi + lax.div(head, 8)
    x = wrap(lax.div(head, 2))
    c = lax.rem(head, 2)
    place = 4 * y + x
    owner = c == y_hi
    up, down, far = wrap(z + 1), wrap(z + 3), wrap(z + 2)
    here_up, here_down = device(x, y, up, c), device(x, y, down, c)
    partner = device(x, y, z, 1 - c)
    across = device(x, wrap(y + 2), z, 1 - c)
    cross = device(x, 3 - y, z, c)

    def remote(src, dst, send, recv, where):
        return pltpu.make_async_remote_copy(
            src_ref=src, dst_ref=dst, send_sem=send, recv_sem=recv,
            device_id=where, device_id_type=MESH,
        )

    def spot(k):
        dx, dy = lax.rem(k, N), lax.div(k, N)
        tx, ty = wrap(x + dx), wrap(y + dy)
        fx, fy = wrap(x + N - dx), wrap(y + N - dy)
        return tx, ty, 4 * ty + tx, 4 * fy + fx

    def stage_copy(k):
        _, _, to, _ = spot(k)
        return pltpu.make_async_copy(
            ckpt_q.at[:, :, pl.ds(pl.multiple_of(to * QCOLS, QCOLS), QCOLS)],
            stage_q.at[k], stage_q_sem.at[k],
        )

    load_k = pltpu.make_async_copy(ckpt_k, stage_kv.at[0], stage_sem.at[0])
    load_v = pltpu.make_async_copy(ckpt_v, stage_kv.at[1], stage_sem.at[1])
    load_o = pltpu.make_async_copy(ckpt_o, stage_o, stage_sem.at[2])
    load_cos = pltpu.make_async_copy(cosine, table.at[0], stage_sem.at[3])
    load_sin = pltpu.make_async_copy(sine, table.at[1], stage_sem.at[4])
    load_k.start()
    load_v.start()

    @pl.loop(0, 16)
    def _(k):
        stage_copy(k).start()

    load_o.start()
    load_cos.start()
    load_sin.start()

    barrier = pltpu.get_barrier_semaphore()

    @pl.loop(1, 16)
    def _(k):
        tx, ty, _, _ = spot(k)
        pl.semaphore_signal(barrier, inc=1, device_id=device(tx, ty, z, c), device_id_type=MESH)

    for peer in (here_up, here_down, partner, across):
        pl.semaphore_signal(barrier, inc=1, device_id=peer, device_id_type=MESH)

    load_k.wait()
    load_v.wait()
    for which in range(2):
        for g in range(8):
            mean_kv[which, g] = average(stage_kv[which, :, :, g * HEAD : (g + 1) * HEAD])

    pl.semaphore_wait(barrier, 19)

    def a2a_copy(k):
        tx, ty, _, _ = spot(k)
        return remote(
            send_w.at[k], weights.at[z, place, c], a2a_send, a2a_recv.at[k], device(tx, ty, z, c)
        )

    def piece(k):
        _, _, to, _ = spot(k)
        stage_copy(k).wait()
        return average(stage_q[k]), mean_kv[lax.rem(to, 2), lax.div(to, 2)]

    side = lax.rem(y, 2)
    inner = device(x, y + 1 - 2 * side, z, c)
    east, west, far_x = wrap(x + 1), wrap(x + 3), wrap(x + 2)

    def strip(ref, at_x, eighth, j):
        start = pl.multiple_of(at_x * PIECE + eighth * (PIECE // 2), PIECE // 2)
        return ref.at[pl.ds((j + 1) * SUB_ROWS, SUB_ROWS), pl.ds(start, PIECE // 2)]

    def top(ref, half, i):
        start = pl.multiple_of((2 * half + i) * PIECE, PIECE)
        return ref.at[pl.ds(0, SUB_ROWS), pl.ds(start, PIECE)]

    def cross_copy(j):
        return remote(
            strip(hidden, x, side, j), strip(hid, x, side, j), cross_send, cross_recv.at[j], cross
        )

    def cross_top(i):
        return remote(
            top(hidden, side, i), top(hid, side, i), cross_send, cross_recv.at[3 + i], cross
        )

    def cross_wait(j):
        block = strip(hid, x, 1 - side, j)
        remote(block, block, cross_send, cross_recv.at[j], cross).wait_recv()

    def inner_copy(j):
        block = strip(hid, x, 1 - side, j)
        return remote(block, block, inner_send, inner_recv.at[j], inner)

    def inner_wait(j):
        block = strip(hid, x, side, j)
        remote(block, block, inner_send, inner_recv.at[j], inner).wait_recv()

    def ring_copy(at_x, eighth, j, direction, slot):
        block = strip(hid, at_x, eighth, j)
        return remote(
            block, block, ring_send, ring_recv.at[slot, eighth, j],
            device(wrap(x + direction), y, z, c),
        )

    def event(number):
        if number < 3:
            cross_wait(number)
            inner_copy(number).start()
            ring_copy(x, 1 - side, number, 1, 0).start()
            ring_copy(x, 1 - side, number, 3, 1).start()
        if 1 <= number < 4:
            inner_wait(number - 1)
            ring_copy(x, side, number - 1, 1, 0).start()
            ring_copy(x, side, number - 1, 3, 1).start()
        if 3 <= number < 5:
            block = top(hid, 1 - side, number - 3)
            remote(block, block, cross_send, cross_recv.at[number], cross).wait_recv()
            remote(block, block, inner_send, inner_recv.at[number], inner).start()
        if 5 <= number < 8:
            j = number - 5

            def far_on(eighth):
                ring_copy(west, eighth, j, 1, 0).wait_recv()
                ring_copy(east, eighth, j, 3, 1).wait_recv()

            far_on(1 - side)
            far_on(side)
            ring_copy(west, 0, j, 1, 2).start()
            ring_copy(east, 1, j, 3, 2).start()

    def events(*numbers):
        @pl.when(jnp.logical_not(owner))
        def _():
            for number in numbers:
                event(number)

    def seg_copy():
        return remote(segments, seg, seg_sem.at[0], seg_sem.at[1], cross)

    local_hid = pltpu.make_async_copy(hidden, hid, hid_sem.at[0])
    local_seg = pltpu.make_async_copy(segments, seg, hid_sem.at[1])

    first_q, first_kv = piece(0)
    weights[z, place, c, :, :QCOLS] = first_q
    weights[z, place, c, :, QCOLS:] = first_kv

    @pl.loop(1, 16)
    def _(k):
        mean_q, mean_pair = piece(k)
        send_w[k, :, :QCOLS] = mean_q
        send_w[k, :, QCOLS:] = mean_pair

        @pl.when(k > 1)
        def _():
            a2a_copy(k - 1).start()

        @pl.when(owner & (lax.rem(k, 5) == 4))
        def _():
            cross_copy(lax.div(k, 5)).start()

    a2a_copy(15).start()

    @pl.when(owner)
    def _():
        cross_top(0).start()
        cross_top(1).start()
        seg_copy().start()
        local_hid.start()
        local_seg.start()

    def z_copy(level, k, direction, send_index, recv_index):
        _, _, _, source = spot(k)
        block = weights.at[level, source, c]
        return remote(
            block, block, z_send.at[send_index], z_recv.at[recv_index, k],
            here_up if direction > 0 else here_down,
        )

    def pair_copy(level, k, slot):
        _, _, _, source = spot(k)
        block = weights.at[level, source, c]
        return remote(block, block, pair_send, pair_recv.at[slot], partner)

    def pair_done(level, slot):
        block = weights.at[level, :, 1 - c]
        return remote(block, block, pair_send, pair_recv.at[slot], partner)

    def a2a_arrival(k):
        _, _, _, source = spot(k)
        block = weights.at[z, source, c]
        return remote(block, block, a2a_send, a2a_recv.at[k], partner)

    def own_part(lo, hi):
        @pl.loop(lo, hi)
        def _(k):
            @pl.when(k > 0)
            def _():
                a2a_arrival(k).wait_recv()

            z_copy(z, k, 1, 0, 0).start()
            z_copy(z, k, -1, 1, 1).start()
            pair_copy(z, k, 0).start()

    own_part(0, 8)

    load_o.wait()
    step = D // 8

    @pl.when(owner)
    def _():
        @pl.loop(0, 8)
        def _(j):
            cols = pl.ds(pl.multiple_of(j * step, step), step)
            weights_o[z, c, :, cols] = average(stage_o[:, :, cols])

    def swap_copy():
        return remote(
            send_o, weights_o.at[z, y_hi], swap_sem.at[0], swap_sem.at[1], across
        )

    @pl.when(jnp.logical_not(owner))
    def _():
        @pl.loop(0, 8)
        def _(j):
            cols = pl.ds(pl.multiple_of(j * step, step), step)
            send_o[:, cols] = average(stage_o[:, :, cols])

    events(0)
    own_part(8, 12)
    events(1)
    own_part(12, 16)
    events(2, 3)

    def pass_on(lo, hi):
        @pl.loop(lo, hi)
        def _(k):
            z_copy(down, k, 1, 0, 0).wait_recv()

            @pl.when(lax.rem(k, 2) == 0)
            def _():
                z_copy(down, k, 1, 0, 2).start()

            pair_copy(down, k, 1).start()
            z_copy(up, k, -1, 1, 1).wait_recv()

            @pl.when(lax.rem(k, 2) == 1)
            def _():
                z_copy(up, k, -1, 1, 2).start()

            pair_copy(up, k, 2).start()

    pass_on(0, 4)
    events(4)
    pass_on(4, 8)
    events(5)
    pass_on(8, 12)
    events(6)
    pass_on(12, 16)
    events(7)

    def o_block(level, core, j):
        return weights_o.at[level, core, :, pl.ds(pl.multiple_of(j * PIECE, PIECE), PIECE)]

    def zo_copy(level, j, direction, send_index, recv_index):
        block = o_block(level, c, j)
        return remote(
            block, block, zo_send.at[send_index], zo_recv.at[recv_index, j],
            here_up if direction > 0 else here_down,
        )

    def pair_o_copy(level, j, slot):
        block = o_block(level, c, j)
        return remote(block, block, pair_o_send, pair_o_recv.at[slot], partner)

    def pair_o_done(level, slot):
        block = weights_o.at[level, 1 - c]
        return remote(block, block, pair_o_send, pair_o_recv.at[slot], partner)

    @pl.when(owner)
    def _():
        local_hid.wait()
        local_seg.wait()

    @pl.when(jnp.logical_not(owner))
    def _():
        swap_copy().start()
        for i in range(2):
            block = top(hid, side, i)
            remote(block, block, inner_send, inner_recv.at[3 + i], inner).wait_recv()

        @pl.loop(0, 3)
        def _(j):
            ring_copy(far_x, 0, j, 1, 2).wait_recv()
            ring_copy(far_x, 1, j, 1, 2).wait_recv()

        seg_copy().wait_recv()

    load_cos.wait()
    load_sin.wait()
    acc[...] = jnp.zeros_like(acc)

    def project(level, lo, hi):
        block = weights[level, :, :, :, lo:hi].reshape(PIECE, hi - lo)
        rows = hid[:, pl.ds(pl.multiple_of(level * PIECE, PIECE), PIECE)]
        acc[:, lo:hi] += jnp.dot(rows, block, preferred_element_type=jnp.float32)

    def rotate(values, rows=slice(None)):
        return values * table[0, rows] + pltpu.roll(values, HEAD // 2, 1) * table[1, rows]

    parity = lax.rem(x, 2)
    kv_peer = device(x + 1 - 2 * parity, y, z, c)
    kv_out = remote(kv.at[parity], kv.at[parity], kv_sem.at[0], kv_sem.at[1], kv_peer)
    kv_in = remote(kv.at[1 - parity], kv.at[1 - parity], kv_sem.at[0], kv_sem.at[1], kv_peer)

    @pl.loop(0, 4)
    def _(i):
        level = wrap(z + jnp.where(i == 1, 3, jnp.where(i == 2, 1, jnp.where(i == 3, 2, 0))))

        @pl.loop(0, 4)
        def _(inner_k):
            k = 4 * i + inner_k
            z_copy(far, k, 1, 0, 2).wait_recv()
            pair_copy(far, k, 3).start()

        @pl.when(i == 3)
        def _():
            @pl.when(jnp.logical_not(owner))
            def _():
                block = weights_o.at[z, c]
                remote(block, block, swap_sem.at[0], swap_sem.at[1], across).wait_recv()

            @pl.loop(0, SUB)
            def _(j):
                zo_copy(z, j, 1, 0, 0).start()
                zo_copy(z, j, -1, 1, 1).start()
                pair_o_copy(z, j, 0).start()

        pair_done(level, i).wait_recv()
        project(level, QCOLS, WCOLS)

        @pl.when(i == 3)
        def _():
            mine = acc[:, QCOLS:]
            kv[parity] = jnp.where(parity == 0, rotate(mine), mine).astype(jnp.bfloat16)
            kv_out.start()

        project(level, 0, QCOLS)

    for h in range(HEADS_CHIP):
        q_rot[h] = rotate(acc[:, h * HEAD : (h + 1) * HEAD]).astype(jnp.bfloat16)
    kv_in.wait_recv()

    segment_row = seg[...].astype(jnp.float32)
    segment_col = jnp.transpose(jnp.broadcast_to(segment_row, (HEAD, TOK)))[:, :1]

    def ctx_copy(part, place_from, h, where, slot):
        block = ctx.at[part, place_from, h]
        return remote(block, block, ctx_send, ctx_recv.at[part, slot, h], where)

    def line(h, along, by):
        on_x = lax.rem(lax.div(h, 2) + along, 2) == 0
        step_x = jnp.where(on_x, by, 0)
        step_y = jnp.where(on_x, 0, by)
        return device(wrap(x + step_x), wrap(y + step_y), z, c)

    def block_at(h, first, second):
        on_x = lax.div(h, 2) == 0
        step_x = jnp.where(on_x, first, second)
        step_y = jnp.where(on_x, second, first)
        return 4 * wrap(y + step_y) + wrap(x + step_x)

    def attend(part):
        rows = slice(part * HALF, (part + 1) * HALF)
        width = (part + 1) * HALF
        row_at = lax.broadcasted_iota(jnp.int32, (HALF, width), 0) + part * HALF
        col_at = lax.broadcasted_iota(jnp.int32, (HALF, width), 1)
        allowed = (row_at >= col_at) & (segment_col[rows] == segment_row[:, :width])

        @pl.loop(0, HEADS_CHIP)
        def _(h):
            scores = lax.dot_general(
                q_rot[h, rows], kv[0, :width], (((1,), (1,)), ((), ())),
                preferred_element_type=jnp.float32,
            ) * HEAD ** (-0.5)
            scores = jnp.where(allowed, scores, -1e30)
            peak = jnp.max(scores, axis=-1, keepdims=True)
            raised = jnp.exp(scores - peak)
            probs = (raised * (1.0 / jnp.sum(raised, axis=-1, keepdims=True))).astype(jnp.bfloat16)
            ctx[part, place, h] = jnp.dot(
                probs, kv[1, :width], preferred_element_type=jnp.float32
            ).astype(jnp.bfloat16)
            ctx_copy(part, place, h, line(h, 0, 1), 1).start()
            ctx_copy(part, place, h, line(h, 0, 3), 3).start()
            ctx_copy(part, place, h, line(h, 1, 1), 4).start()
            ctx_copy(part, place, h, line(h, 1, 3), 12).start()

    def ctx_wait(part, h, first, second, slot):
        block = ctx.at[part, block_at(h, first, second), h]
        remote(block, block, ctx_send, ctx_recv.at[part, slot, h], partner).wait_recv()

    def onward(part, h, slot):
        source = block_at(h, 4 - slot, 0)

        @pl.when(lax.rem(h, 2) == (0 if slot == 1 else 1))
        def _():
            ctx_copy(part, source, h, line(h, 0, slot), 2).start()

        ctx_copy(part, source, h, line(h, 1, 1), 4 + slot).start()
        ctx_copy(part, source, h, line(h, 1, 3), 12 + slot).start()

    def first_axis(part):
        @pl.loop(0, HEADS_CHIP)
        def _(h):
            ctx_wait(part, h, 3, 0, 1)
            onward(part, h, 1)
            ctx_wait(part, h, 1, 0, 3)
            onward(part, h, 3)

    def first_axis_far(part):
        @pl.loop(0, HEADS_CHIP)
        def _(h):
            ctx_wait(part, h, 2, 0, 2)
            source = block_at(h, 2, 0)
            ctx_copy(part, source, h, line(h, 1, 1), 4 + 2).start()
            ctx_copy(part, source, h, line(h, 1, 3), 12 + 2).start()

    def second_axis(part, lo, hi):
        @pl.loop(lo, hi)
        def _(i):
            t = jnp.where(i == 2, 3, jnp.where(i == 3, 2, i))
            first = wrap(N - t)

            @pl.loop(0, HEADS_CHIP)
            def _(h):
                even = lax.rem(h, 2) == 0
                ctx_wait(part, h, first, 3, 4 + t)

                @pl.when(even)
                def _():
                    ctx_copy(part, block_at(h, first, 3), h, line(h, 1, 1), 8 + t).start()

                ctx_wait(part, h, first, 1, 12 + t)

                @pl.when(jnp.logical_not(even))
                def _():
                    ctx_copy(part, block_at(h, first, 1), h, line(h, 1, 3), 8 + t).start()

    def second_axis_far(part):
        @pl.loop(0, 4)
        def _(t):
            @pl.loop(0, HEADS_CHIP)
            def _(h):
                ctx_wait(part, h, wrap(N - t), 2, 8 + t)

    def rows_on(lo, hi):
        @pl.loop(lo, hi)
        def _(j):
            zo_copy(down, j, 1, 0, 0).wait_recv()

            @pl.when(lax.rem(j, 2) == 0)
            def _():
                zo_copy(down, j, 1, 0, 2).start()

            pair_o_copy(down, j, 1).start()
            zo_copy(up, j, -1, 1, 1).wait_recv()

            @pl.when(lax.rem(j, 2) == 1)
            def _():
                zo_copy(up, j, -1, 1, 2).start()

            pair_o_copy(up, j, 2).start()

    def combine(part, offsets):
        rows = pl.ds(part * HALF, HALF)

        @pl.loop(0, len(offsets))
        def _(i):
            offset = offsets[0]
            for at in range(1, len(offsets)):
                offset = jnp.where(i == at, offsets[at], offset)
            places = [(4 * wrap(y + offset) + along, 0) for along in range(N)]
            places += [(4 * along + wrap(x + offset), 2) for along in range(N)]
            left = jnp.concatenate(
                [ctx[part, p, first + h] for p, first in places for h in range(2)], axis=1
            )
            right = jnp.concatenate(
                [
                    weights_o[
                        :, :, :,
                        pl.ds(pl.multiple_of(p * QCOLS + first * HEAD, 2 * HEAD), 2 * HEAD),
                    ].reshape(TOK, 2 * HEAD)
                    for p, first in places
                ],
                axis=1,
            )
            acc[rows, :QCOLS] += lax.dot_general(
                left, right, (((1,), (1,)), ((), ())), preferred_element_type=jnp.float32
            )

    def deliver(part):
        rows = pl.ds(part * HALF, HALF)
        out_block[part] = acc[rows, :QCOLS].astype(jnp.bfloat16)

        @pl.when(owner)
        def _():
            pltpu.make_async_copy(out_block.at[part], out.at[rows], stay_sem.at[part]).start()

        @pl.when(jnp.logical_not(owner))
        def _():
            leave_copy(part).start()

    def leave_copy(part):
        rows = pl.ds(part * HALF, HALF)
        return remote(
            out_block.at[part], out.at[rows], leave_send.at[part], leave_recv.at[part], across
        )

    attend(0)
    attend(1)
    acc[:, :QCOLS] = jnp.zeros((TOK, QCOLS), jnp.float32)
    first_axis(0)
    rows_on(0, 2)
    first_axis_far(0)
    first_axis(1)
    second_axis(0, 0, 2)
    rows_on(2, 4)
    second_axis(0, 2, 4)
    first_axis_far(1)
    second_axis_far(0)

    @pl.loop(0, SUB)
    def _(j):
        zo_copy(far, j, 1, 0, 2).wait_recv()
        pair_o_copy(far, j, 3).start()

    second_axis(1, 0, 1)
    pair_o_done(z, 0).wait_recv()
    pair_o_done(down, 1).wait_recv()
    pair_o_done(up, 2).wait_recv()
    pair_o_done(far, 3).wait_recv()
    combine(0, (0, 1))
    second_axis(1, 1, 2)
    combine(0, (3, 2))
    deliver(0)
    second_axis(1, 2, 4)
    combine(1, (0, 1, 3))
    second_axis_far(1)
    combine(1, (2,))
    deliver(1)

    @pl.when(owner)
    def _():
        for part in range(2):
            rows = pl.ds(part * HALF, HALF)
            pltpu.make_async_copy(out_block.at[part], out.at[rows], stay_sem.at[part]).wait()

    @pl.when(jnp.logical_not(owner))
    def _():
        for part in range(2):
            leave_copy(part).wait()

    def drained(ref, sem):
        remote(ref, ref, sem, kv_sem.at[1], partner).wait_send()

    drained(weights.at[0, pl.ds(0, 15), 0], a2a_send)
    for direction in range(2):
        drained(weights.at[0, pl.ds(0, 12)], z_send.at[direction])
        drained(weights_o.at[pl.ds(0, 3), 0, :, pl.ds(0, 2 * PIECE)], zo_send.at[direction])
    drained(weights.at[:, :, 0], pair_send)
    drained(weights_o.at[:, 0], pair_o_send)
    drained(kv.at[0], kv_sem.at[0])
    drained(ctx.at[:, pl.ds(0, 15)], ctx_send)

    @pl.when(owner)
    def _():
        drained(hid.at[pl.ds(0, SUB_ROWS), pl.ds(0, 7 * PIECE // 2)], cross_send)
        drained(seg, seg_sem.at[0])

    @pl.when(jnp.logical_not(owner))
    def _():
        drained(hid.at[pl.ds(0, SUB_ROWS), pl.ds(0, 7 * PIECE // 2)], inner_send)
        drained(hid.at[pl.ds(0, 3 * SUB_ROWS), pl.ds(0, 3 * PIECE)], ring_send)
        drained(send_o, swap_sem.at[0])


def tables():
    half = HEAD // 2
    freq = np.float32(rope_base) ** (
        np.float32(-2.0) * np.arange(half, dtype=np.float32) / np.float32(HEAD)
    )
    angle = np.arange(TOK, dtype=np.float32)[:, None] * freq.astype(np.float32)[None, :]
    cosine, sine = np.cos(angle), np.sin(angle)
    return (
        np.concatenate([cosine, cosine], axis=1).astype(np.float32),
        np.concatenate([-sine, sine], axis=1).astype(np.float32),
    )


def shards(ckpt_query, ckpt_key, ckpt_value, ckpt_output, hidden_in, segment_ids):
    bf16, f32 = jnp.bfloat16, jnp.float32
    dma = pltpu.SemaphoreType.DMA
    cosine, sine = tables()
    anywhere = pl.BlockSpec(memory_space=pl.ANY)
    return pl.pallas_call(
        kernel,
        out_shape=jax.ShapeDtypeStruct((TOK, TOK), bf16),
        in_specs=[anywhere] * 8,
        out_specs=anywhere,
        scratch_shapes=[
            pltpu.VMEM((16, 4, ROWS, QCOLS), bf16),
            pltpu.VMEM((2, 4, ROWS, 1024), bf16),
            pltpu.VMEM((4, ROWS, D), bf16),
            pltpu.VMEM((2, 8, ROWS, HEAD), bf16),
            pltpu.VMEM((16, ROWS, WCOLS), bf16),
            pltpu.VMEM((ROWS, D), bf16),
            pltpu.VMEM((4, 16, 2, ROWS, WCOLS), bf16),
            pltpu.VMEM((TOK, D), bf16),
            pltpu.VMEM((TOK, WCOLS), f32),
            pltpu.VMEM((4, 2, ROWS, D), bf16),
            pltpu.VMEM((2, 16, HEADS_CHIP, HALF, HEAD), bf16),
            pltpu.VMEM((HEADS_CHIP, TOK, HEAD), bf16),
            pltpu.VMEM((2, TOK, HEAD), bf16),
            pltpu.VMEM((1, TOK), jnp.int32),
            pltpu.VMEM((2, TOK, HEAD), f32),
            pltpu.VMEM((2, HALF, TOK), bf16),
            dma((16,)),
            dma((5,)),
            dma,
            dma((16,)),
            dma((2,)),
            dma((3, 16)),
            dma,
            dma((4,)),
            dma((2,)),
            dma,
            dma((5,)),
            dma,
            dma((5,)),
            dma,
            dma((3, 2, 3)),
            dma((2,)),
            dma((2,)),
            dma((2,)),
            dma((2,)),
            dma((3, SUB)),
            dma,
            dma((4,)),
            dma,
            dma((2, 16, HEADS_CHIP)),
            dma((2,)),
            dma((2,)),
            dma((2,)),
        ],
        compiler_params=pltpu.CompilerParams(
            collective_id=0, has_side_effects=True, vmem_limit_bytes=66_000_000
        ),
    )(ckpt_query, ckpt_key, ckpt_value, ckpt_output, hidden_in, segment_ids, cosine, sine)


def solution(mesh):
    placed = (
        P(None, ("dp", "head"), None),
        P(None, ("dp", "head"), None),
        P(None, ("dp", "head"), None),
        P(None, ("head", "dp"), None),
        P("dp", None),
        P("dp", None),
    )
    return jax.shard_map(
        shards, mesh=mesh, in_specs=placed, out_specs=P("dp", "head"), check_vma=False
    )
```

time: 154 us -> 132 us (0.86); the launches traced: 152 us -> 132 us
  Pallas kernels: 150 us -> 130 us
    pallas_call x1, Pallas kernels: 150 us -> 130 us  [shards(): pl.pallas_call(kernel, out_shape=jax.ShapeDtypeStruct((TOK, TOK), bf16),...]
where the time goes in v3:
time: 132 us
  Pallas kernels  130 us (98%)
  local copies, waits for them, and re-layouts  1.87 us (1%)
    pallas_call x1, Pallas kernels, shards(): pl.pallas_call(kernel, out_shape=jax.ShapeDtypeStruct((TOK, TOK), bf16),...  130 us

profile of v3, /device:TPU:1, one launch (start us, length us, event | category | flops | bytes accessed | tf_op | source)
XLA Modules:
  0.0 131.7 jit_solution(6128617193154515810)
XLA Ops:
  0.0 129.8 %shard_map.82 = bf16[512,512]{1,0:T(8,128)(2,1)} custom-call(bf16[4,64,8192]{2,1,0:T(8,128)(2,1)} %ckpt_q.1, bf16[4,64,1024]{2,1,0:T(8,128)(2,1)} %ckpt_k.1, bf16[4,64,1024]{2,1,0:T(8,128)(2,1)} %ckpt_v.1, bf16[4,64,8192]{2,1,0:T(8,128)(2,1)} %ckpt_o.1, bf16[512,8192]{1,0:T(8,128)(2,1)} %hidden.1, s32[1,512]{1,0:T(1,128)} %segments.1, ...), custom_call_target="tpu_custom_call" | custom-call | tf_op jit(solution)/shard_map/pallas_call | solution.py:667
  129.8 1.9 %copy.10 = bf16[512,512]{1,0:T(8,128)(2,1)} copy(bf16[512,512]{1,0:T(8,128)(2,1)} %shard_map.82) | data formatting | bytes 1048576

commit v4 on v3

--- a/solution.py
+++ b/solution.py
@@ -21,7 +21,8 @@
 SUB = 4
 PIECE = D // N
 SUB_ROWS = TOK // 4
-HALF = TOK // 2
+START = (0, 384)
+SIZE = (384, 128)
 
 
 def average(stack):
@@ -417,7 +418,7 @@
     segment_col = jnp.transpose(jnp.broadcast_to(segment_row, (HEAD, TOK)))[:, :1]
 
     def ctx_copy(part, place_from, h, where, slot):
-        block = ctx.at[part, place_from, h]
+        block = ctx.at[place_from, h, pl.ds(START[part], SIZE[part])]
         return remote(block, block, ctx_send, ctx_recv.at[part, slot, h], where)
 
     def line(h, along, by):
@@ -433,10 +434,10 @@
         return 4 * wrap(y + step_y) + wrap(x + step_x)
 
     def attend(part):
-        rows = slice(part * HALF, (part + 1) * HALF)
-        width = (part + 1) * HALF
-        row_at = lax.broadcasted_iota(jnp.int32, (HALF, width), 0) + part * HALF
-        col_at = lax.broadcasted_iota(jnp.int32, (HALF, width), 1)
+        width = START[part] + SIZE[part]
+        rows = slice(START[part], width)
+        row_at = lax.broadcasted_iota(jnp.int32, (SIZE[part], width), 0) + START[part]
+        col_at = lax.broadcasted_iota(jnp.int32, (SIZE[part], width), 1)
         allowed = (row_at >= col_at) & (segment_col[rows] == segment_row[:, :width])
 
         @pl.loop(0, HEADS_CHIP)
@@ -449,7 +450,7 @@
             peak = jnp.max(scores, axis=-1, keepdims=True)
             raised = jnp.exp(scores - peak)
             probs = (raised * (1.0 / jnp.sum(raised, axis=-1, keepdims=True))).astype(jnp.bfloat16)
-            ctx[part, place, h] = jnp.dot(
+            ctx[place, h, rows] = jnp.dot(
                 probs, kv[1, :width], preferred_element_type=jnp.float32
             ).astype(jnp.bfloat16)
             ctx_copy(part, place, h, line(h, 0, 1), 1).start()
@@ -458,7 +459,7 @@
             ctx_copy(part, place, h, line(h, 1, 3), 12).start()
 
     def ctx_wait(part, h, first, second, slot):
-        block = ctx.at[part, block_at(h, first, second), h]
+        block = ctx.at[block_at(h, first, second), h, pl.ds(START[part], SIZE[part])]
         remote(block, block, ctx_send, ctx_recv.at[part, slot, h], partner).wait_recv()
 
     def onward(part, h, slot):
@@ -534,7 +535,7 @@
             pair_o_copy(up, j, 2).start()
 
     def combine(part, offsets):
-        rows = pl.ds(part * HALF, HALF)
+        rows = pl.ds(START[part], SIZE[part])
 
         @pl.loop(0, len(offsets))
         def _(i):
@@ -544,7 +545,7 @@
             places = [(4 * wrap(y + offset) + along, 0) for along in range(N)]
             places += [(4 * along + wrap(x + offset), 2) for along in range(N)]
             left = jnp.concatenate(
-                [ctx[part, p, first + h] for p, first in places for h in range(2)], axis=1
+                [ctx[p, first + h, rows] for p, first in places for h in range(2)], axis=1
             )
             right = jnp.concatenate(
                 [
@@ -561,21 +562,21 @@
             )
 
     def deliver(part):
-        rows = pl.ds(part * HALF, HALF)
-        out_block[part] = acc[rows, :QCOLS].astype(jnp.bfloat16)
+        rows = pl.ds(START[part], SIZE[part])
+        out_block[rows] = acc[rows, :QCOLS].astype(jnp.bfloat16)
 
         @pl.when(owner)
         def _():
-            pltpu.make_async_copy(out_block.at[part], out.at[rows], stay_sem.at[part]).start()
+            pltpu.make_async_copy(out_block.at[rows], out.at[rows], stay_sem.at[part]).start()
 
         @pl.when(jnp.logical_not(owner))
         def _():
             leave_copy(part).start()
 
     def leave_copy(part):
-        rows = pl.ds(part * HALF, HALF)
+        rows = pl.ds(START[part], SIZE[part])
         return remote(
-            out_block.at[part], out.at[rows], leave_send.at[part], leave_recv.at[part], across
+            out_block.at[rows], out.at[rows], leave_send.at[part], leave_recv.at[part], across
         )
 
     attend(0)
@@ -614,8 +615,8 @@
     @pl.when(owner)
     def _():
         for part in range(2):
-            rows = pl.ds(part * HALF, HALF)
-            pltpu.make_async_copy(out_block.at[part], out.at[rows], stay_sem.at[part]).wait()
+            rows = pl.ds(START[part], SIZE[part])
+            pltpu.make_async_copy(out_block.at[rows], out.at[rows], stay_sem.at[part]).wait()
 
     @pl.when(jnp.logical_not(owner))
     def _():
@@ -632,7 +633,7 @@
     drained(weights.at[:, :, 0], pair_send)
     drained(weights_o.at[:, 0], pair_o_send)
     drained(kv.at[0], kv_sem.at[0])
-    drained(ctx.at[:, pl.ds(0, 15)], ctx_send)
+    drained(ctx.at[pl.ds(0, 15)], ctx_send)
 
     @pl.when(owner)
     def _():
@@ -680,12 +681,12 @@
             pltpu.VMEM((TOK, D), bf16),
             pltpu.VMEM((TOK, WCOLS), f32),
             pltpu.VMEM((4, 2, ROWS, D), bf16),
-            pltpu.VMEM((2, 16, HEADS_CHIP, HALF, HEAD), bf16),
+            pltpu.VMEM((16, HEADS_CHIP, TOK, HEAD), bf16),
             pltpu.VMEM((HEADS_CHIP, TOK, HEAD), bf16),
             pltpu.VMEM((2, TOK, HEAD), bf16),
             pltpu.VMEM((1, TOK), jnp.int32),
             pltpu.VMEM((2, TOK, HEAD), f32),
-            pltpu.VMEM((2, HALF, TOK), bf16),
+            pltpu.VMEM((TOK, TOK), bf16),
             dma((16,)),
             dma((5,)),
             dma,

time: 132 us -> 135 us (1.023)
  Pallas kernels: 130 us -> 133 us
    pallas_call x1, Pallas kernels: 130 us -> 133 us  [shards(): pl.pallas_call(kernel, out_shape=jax.ShapeDtypeStruct((TOK, TOK), bf16),...]
where the time goes in v4:
time: 135 us
  Pallas kernels  133 us (99%)
  local copies, waits for them, and re-layouts  1.87 us (1%)
    pallas_call x1, Pallas kernels, shards(): pl.pallas_call(kernel, out_shape=jax.ShapeDtypeStruct((TOK, TOK), bf16),...  133 us

profile of v4, /device:TPU:1, one launch (start us, length us, event | category | flops | bytes accessed | tf_op | source)
XLA Modules:
  0.0 134.6 jit_solution(11461528049268692278)
XLA Ops:
  0.0 132.7 %shard_map.82 = bf16[512,512]{1,0:T(8,128)(2,1)} custom-call(bf16[4,64,8192]{2,1,0:T(8,128)(2,1)} %ckpt_q.1, bf16[4,64,1024]{2,1,0:T(8,128)(2,1)} %ckpt_k.1, bf16[4,64,1024]{2,1,0:T(8,128)(2,1)} %ckpt_v.1, bf16[4,64,8192]{2,1,0:T(8,128)(2,1)} %ckpt_o.1, bf16[512,8192]{1,0:T(8,128)(2,1)} %hidden.1, s32[1,512]{1,0:T(1,128)} %segments.1, ...), custom_call_target="tpu_custom_call" | custom-call | tf_op jit(solution)/shard_map/pallas_call | solution.py:668
  132.7 1.9 %copy.10 = bf16[512,512]{1,0:T(8,128)(2,1)} copy(bf16[512,512]{1,0:T(8,128)(2,1)} %shard_map.82) | data formatting | bytes 1048576

commit v5 on v4

--- a/solution.py
+++ b/solution.py
@@ -21,8 +21,8 @@
 SUB = 4
 PIECE = D // N
 SUB_ROWS = TOK // 4
-START = (0, 384)
-SIZE = (384, 128)
+START = (0, 192)
+SIZE = (192, 320)
 
 
 def average(stack):
@@ -580,9 +580,9 @@
         )
 
     attend(0)
+    first_axis(0)
     attend(1)
     acc[:, :QCOLS] = jnp.zeros((TOK, QCOLS), jnp.float32)
-    first_axis(0)
     rows_on(0, 2)
     first_axis_far(0)
     first_axis(1)

time: 135 us -> 131 us (0.970)
  Pallas kernels: 133 us -> 129 us
    pallas_call x1, Pallas kernels: 133 us -> 129 us  [shards(): pl.pallas_call(kernel, out_shape=jax.ShapeDtypeStruct((TOK, TOK), bf16),...]
where the time goes in v5:
time: 131 us
  Pallas kernels  129 us (98%)
  local copies, waits for them, and re-layouts  1.87 us (1%)
    pallas_call x1, Pallas kernels, shards(): pl.pallas_call(kernel, out_shape=jax.ShapeDtypeStruct((TOK, TOK), bf16),...  129 us

profile of v5, /device:TPU:1, one launch (start us, length us, event | category | flops | bytes accessed | tf_op | source)
XLA Modules:
  0.0 130.9 jit_solution(1689163877035843536)
XLA Ops:
  0.0 129.0 %shard_map.82 = bf16[512,512]{1,0:T(8,128)(2,1)} custom-call(bf16[4,64,8192]{2,1,0:T(8,128)(2,1)} %ckpt_q.1, bf16[4,64,1024]{2,1,0:T(8,128)(2,1)} %ckpt_k.1, bf16[4,64,1024]{2,1,0:T(8,128)(2,1)} %ckpt_v.1, bf16[4,64,8192]{2,1,0:T(8,128)(2,1)} %ckpt_o.1, bf16[512,8192]{1,0:T(8,128)(2,1)} %hidden.1, s32[1,512]{1,0:T(1,128)} %segments.1, ...), custom_call_target="tpu_custom_call" | custom-call | tf_op jit(solution)/shard_map/pallas_call | solution.py:668
  129.0 1.9 %copy.10 = bf16[512,512]{1,0:T(8,128)(2,1)} copy(bf16[512,512]{1,0:T(8,128)(2,1)} %shard_map.82) | data formatting | bytes 1048576

commit v6 on v5

--- a/solution.py
+++ b/solution.py
@@ -21,8 +21,8 @@
 SUB = 4
 PIECE = D // N
 SUB_ROWS = TOK // 4
-START = (0, 192)
-SIZE = (192, 320)
+START = (0, 128)
+SIZE = (128, 384)
 
 
 def average(stack):

time: 131 us -> 130 us (level)
  no operation moved by 1% of the time
where the time goes in v6:
time: 130 us
  Pallas kernels  128 us (98%)
  local copies, waits for them, and re-layouts  1.87 us (1%)
    pallas_call x1, Pallas kernels, shards(): pl.pallas_call(kernel, out_shape=jax.ShapeDtypeStruct((TOK, TOK), bf16),...  128 us

profile of v6, /device:TPU:1, one launch (start us, length us, event | category | flops | bytes accessed | tf_op | source)
XLA Modules:
  0.0 129.9 jit_solution(1985013894245831190)
XLA Ops:
  0.0 128.0 %shard_map.82 = bf16[512,512]{1,0:T(8,128)(2,1)} custom-call(bf16[4,64,8192]{2,1,0:T(8,128)(2,1)} %ckpt_q.1, bf16[4,64,1024]{2,1,0:T(8,128)(2,1)} %ckpt_k.1, bf16[4,64,1024]{2,1,0:T(8,128)(2,1)} %ckpt_v.1, bf16[4,64,8192]{2,1,0:T(8,128)(2,1)} %ckpt_o.1, bf16[512,8192]{1,0:T(8,128)(2,1)} %hidden.1, s32[1,512]{1,0:T(1,128)} %segments.1, ...), custom_call_target="tpu_custom_call" | custom-call | tf_op jit(solution)/shard_map/pallas_call | solution.py:668
  128.0 1.9 %copy.10 = bf16[512,512]{1,0:T(8,128)(2,1)} copy(bf16[512,512]{1,0:T(8,128)(2,1)} %shard_map.82) | data formatting | bytes 1048576
